TPU v7x, 32 devices: a whole 2x2x4 slice. The times are simulated.
32 devices in a mesh: dp: 4 (over y, x), row: 4 (over z), col: 2 (over core).
Axes of the slice: x: 2, y: 2, z: 4, core: 2. Of those that a mesh axis runs over, the one named last changes fastest.
Arguments:
- tokens: bfloat16 [16384, 768], P(('dp', 'row'), 'col'), may hold values from -6 to 6
- cotangent: bfloat16 [16384, 768], P(('dp', 'row'), 'col'), may hold values from -6 to 6
- qkv_weight: float32 [3, 768, 768], P(None, ('dp', 'row'), 'col'), may hold values from -0.3125 to 0.3125
- out_weight: float32 [768, 768], P('col', ('dp', 'row')), may hold values from -1.75 to 1.75
- up_weight: float32 [768, 3072], P(('dp', 'row'), 'col'), may hold values from -0.21875 to 0.21875
- down_weight: float32 [3072, 768], P('col', ('dp', 'row')), may hold values from -0.21875 to 0.21875
- query_bias: float32 [768], P('col'), may hold values from -3 to 3
- value_bias: float32 [768], P('col'), may hold values from -3 to 3
- out_bias: float32 [768], replicated, may hold values from -3 to 3
- up_bias: float32 [3072], P('col'), may hold values from -3 to 3
- down_bias: float32 [768], replicated, may hold values from -3 to 3
- first_gain: float32 [768], replicated, may hold values from 0.5 to 1.5
- first_shift: float32 [768], replicated, may hold values from -3 to 3
- second_gain: float32 [768], replicated, may hold values from 0.5 to 1.5
- second_shift: float32 [768], replicated, may hold values from -3 to 3
- head_gate: int32 [12], P('col'), may hold values from 0 to 1, as said below
- hidden_gate: int32 [768], replicated, may hold values 0 or 1
- intermediate_gate: int32 [3072], P('col'), may hold values 0 or 1
- attention_gate: int32 [16], P(('dp', 'row')), may hold values 0 or 1
- feedforward_gate: int32 [16], P(('dp', 'row')), may hold values 0 or 1
- prefix_length: int32 [16], P(('dp', 'row')), may hold values from 102 to 512
Outputs:
- layer_out: float32 [16384, 768], P(('dp', 'row'), 'col')
- grad_tokens: float32 [16384, 768], P(('dp', 'row'), 'col')
- grad_qkv: float32 [3, 768, 768], P(None, ('dp', 'row'), 'col')
- grad_out: float32 [768, 768], P('col', ('dp', 'row'))
- grad_up: float32 [768, 3072], P(('dp', 'row'), 'col')
- grad_down: float32 [3072, 768], P('col', ('dp', 'row'))
- grad_query_bias: float32 [768], P('col')
- grad_value_bias: float32 [768], P('col')
- grad_out_bias: float32 [768], replicated
- grad_up_bias: float32 [3072], P('col')
- grad_down_bias: float32 [768], replicated
- grad_first_gain: float32 [768], replicated
- grad_first_shift: float32 [768], replicated
- grad_second_gain: float32 [768], replicated
- grad_second_shift: float32 [768], replicated
- grad_head_gate: float32 [12], P('col')
- grad_hidden_gate: float32 [768], replicated
- grad_unit_gate: float32 [3072], P('col')
- grad_attention_gate: float32 [16], replicated
- grad_feedforward_gate: float32 [16], replicated
Inputs may be any that keep to these rules, and one draw needn't show every extreme that they name: `head_gate`: 1 keeps a head, 0 removes it; exactly 3 heads are removed. `hidden_gate`: 1 keeps a feature on both branch outputs, 0 removes it. `intermediate_gate`: 1 keeps a hidden unit, 0 removes it. `attention_gate`: 1 keeps the sequence's attention sub-layer, 0 removes it. `feedforward_gate`: 1 keeps the sequence's feed-forward sub-layer, 0 removes it. `prefix_length`: positions below a sequence's prefix length see each other both ways.
All inputs are finite; a program needn't handle non-finite values. No bound on the sum of `intermediate_gate` or of `attention_gate` or of `feedforward_gate` on one device may be relied on, other than what follows from the above.
Results may differ from a plain program's by a relative error of at most 0.015.
The roundings to bfloat16 on the way count: a program that leaves them out, or rounds other values in their place, can miss the bound.
Values may be sent and summed in bfloat16 or wider, within the bound.
A program may use at most 128 MiB of HBM per device.

v0:
```python
from functools import partial
import math
from typing import NamedTuple

import jax
import jax.numpy as jnp
from jax import lax
from jax.experimental import pallas as pl
from jax.experimental.pallas import tpu as pltpu
from jax.sharding import PartitionSpec as P

masked_value = -1e30
norm_eps = 1e-05


def norm_forward(values, scale_gain, shift_term):
    centre = jnp.mean(values, axis=1, keepdims=True)
    centred = values - centre
    spread = jnp.mean(centred * centred, axis=1, keepdims=True)
    inverse = lax.rsqrt(spread + norm_eps)
    normed = centred * inverse
    return (normed * scale_gain + shift_term, normed, inverse)


def norm_backward(gradient, normed, inverse, scale_gain):
    scaled = gradient * scale_gain
    first_mean = jnp.mean(scaled, axis=1, keepdims=True)
    second_mean = jnp.mean(scaled * normed, axis=1, keepdims=True)
    return inverse * (scaled - first_mean - normed * second_mean)


def block_mask(start_row, block_rows, length, prefix_value):
    key_index = jnp.arange(length, dtype=jnp.int32)
    query_index = start_row + jnp.arange(block_rows, dtype=jnp.int32)
    return (key_index[None, :] < prefix_value) | (key_index[None, :] <= query_index[:, None])


def block_scores(query_block, key_seq, start_row, prefix_value, scale_factor):
    block_rows = query_block.shape[0]
    length = key_seq.shape[0]
    allowed = block_mask(start_row, block_rows, length, prefix_value)
    scores = (
        jnp.einsum("qhd,khd->hqk", query_block, key_seq, preferred_element_type=jnp.float32)
        * scale_factor
    )
    return jnp.where(allowed[None], scores, masked_value)


def attend_sequence(query_seq, key_seq, value_seq, prefix_value, block_rows, scale_factor):
    length = key_seq.shape[0]
    block_count = length // block_rows
    query_blocks = query_seq.reshape(
        block_count, block_rows, query_seq.shape[1], query_seq.shape[2]
    )
    starts = jnp.arange(block_count, dtype=jnp.int32) * block_rows

    def one_block(element):
        query_block, start_row = element
        scores = block_scores(query_block, key_seq, start_row, prefix_value, scale_factor)
        row_peak = jnp.max(scores, axis=2, keepdims=True)
        exponent = jnp.exp(scores - row_peak)
        row_total = jnp.sum(exponent, axis=2, keepdims=True)
        weights_low = (exponent / row_total).astype(jnp.bfloat16)
        context = jnp.einsum(
            "hqk,khd->qhd", weights_low, value_seq, preferred_element_type=jnp.float32
        )
        return (context, row_peak[..., 0] + jnp.log(row_total[..., 0]))

    contexts, log_totals = lax.map(one_block, (query_blocks, starts))
    return (contexts.reshape(length, query_seq.shape[1], query_seq.shape[2]), log_totals)


def attend_back(
    query_seq, key_seq, value_seq, grad_seq, log_seq, prefix_value, block_rows, scale_factor
):
    length = key_seq.shape[0]
    block_count = length // block_rows
    head_count = query_seq.shape[1]
    head_size = query_seq.shape[2]
    query_blocks = query_seq.reshape(block_count, block_rows, head_count, head_size)
    grad_blocks = grad_seq.reshape(block_count, block_rows, head_count, head_size)
    starts = jnp.arange(block_count, dtype=jnp.int32) * block_rows

    def one_block(running, element):
        grad_keys, grad_values = running
        query_block, grad_block, log_block, start_row = element
        scores = block_scores(query_block, key_seq, start_row, prefix_value, scale_factor)
        probs = jnp.exp(scores - log_block[..., None])
        grad_probs = jnp.einsum(
            "qhd,khd->hqk", grad_block, value_seq, preferred_element_type=jnp.float32
        )
        row_inner = jnp.sum(probs * grad_probs, axis=2, keepdims=True)
        grad_scores = (probs * (grad_probs - row_inner)).astype(jnp.bfloat16)
        grad_query = (
            jnp.einsum("hqk,khd->qhd", grad_scores, key_seq, preferred_element_type=jnp.float32)
            * scale_factor
        )
        grad_keys = (
            grad_keys
            + jnp.einsum(
                "hqk,qhd->khd", grad_scores, query_block, preferred_element_type=jnp.float32
            )
            * scale_factor
        )
        grad_values = grad_values + jnp.einsum(
            "hqk,qhd->khd",
            probs.astype(jnp.bfloat16),
            grad_block,
            preferred_element_type=jnp.float32,
        )
        return ((grad_keys, grad_values), grad_query)

    zeros_kv = jnp.zeros((length, head_count, head_size), jnp.float32)
    (grad_keys, grad_values), grad_query = lax.scan(
        one_block, (zeros_kv, zeros_kv), (query_blocks, grad_blocks, log_seq, starts)
    )
    return (grad_query.reshape(length, head_count, head_size), grad_keys, grad_values)


def per_device(
    tokens,
    cotangent,
    qkv_weight,
    out_weight,
    up_weight,
    down_weight,
    query_bias,
    value_bias,
    out_bias,
    up_bias,
    down_bias,
    first_gain,
    first_shift,
    second_gain,
    second_shift,
    head_gate,
    hidden_gate,
    intermediate_gate,
    attention_gate,
    feedforward_gate,
    prefix_length,
):
    row_count = tokens.shape[0]
    seq_count = prefix_length.shape[0]
    length = row_count // seq_count
    local_heads = head_gate.shape[0]
    head_width = qkv_weight.shape[2]
    head_size = head_width // local_heads
    model_width = first_gain.shape[0]
    part_width = model_width // lax.axis_size("col")
    block_rows = min(512, length)
    scale_factor = head_size ** (-0.5)
    col_index = lax.axis_index("col")
    qkv_low, out_low = (
        lax.all_gather(qkv_weight.astype(jnp.bfloat16), ("dp", "row"), axis=1, tiled=True),
        lax.all_gather(out_weight.astype(jnp.bfloat16), ("dp", "row"), axis=1, tiled=True),
    )
    up_low, down_low = (
        lax.all_gather(up_weight.astype(jnp.bfloat16), ("dp", "row"), axis=0, tiled=True),
        lax.all_gather(down_weight.astype(jnp.bfloat16), ("dp", "row"), axis=1, tiled=True),
    )
    token_full = lax.all_gather(tokens, "col", axis=1, tiled=True)
    projected = jnp.einsum("td,kdf->ktf", token_full, qkv_low, preferred_element_type=jnp.float32)
    query_low = (projected[0] + query_bias).astype(jnp.bfloat16)
    key_low = projected[1].astype(jnp.bfloat16)
    value_low = (projected[2] + value_bias).astype(jnp.bfloat16)

    def split_heads(array):
        return array.reshape(seq_count, length, local_heads, head_size)

    def forward_seq(element):
        query_seq, key_seq, value_seq, prefix_value = element
        return attend_sequence(
            query_seq, key_seq, value_seq, prefix_value, block_rows, scale_factor
        )

    contexts, log_totals = lax.map(
        forward_seq,
        (split_heads(query_low), split_heads(key_low), split_heads(value_low), prefix_length),
    )
    context = contexts.reshape(row_count, head_width)
    gate_columns = jnp.repeat(head_gate.astype(jnp.float32), head_size)
    gated_low = (context * gate_columns).astype(jnp.bfloat16)
    attn_terms = jnp.dot(gated_low, out_low, preferred_element_type=jnp.float32)
    attn_out = lax.psum(attn_terms, "col") + out_bias
    hidden_mask = hidden_gate.astype(jnp.float32)
    attn_rows = jnp.repeat(attention_gate.astype(jnp.float32), length)[:, None]
    dense_rows = jnp.repeat(feedforward_gate.astype(jnp.float32), length)[:, None]
    first_sum = token_full.astype(jnp.float32) + attn_rows * hidden_mask * attn_out
    normed_one, first_normed, first_inverse = norm_forward(first_sum, first_gain, first_shift)
    normed_low = normed_one.astype(jnp.bfloat16)
    pre_act = jnp.dot(normed_low, up_low, preferred_element_type=jnp.float32) + up_bias
    activated, gelu_pull = jax.vjp(partial(jax.nn.gelu, approximate=False), pre_act)
    unit_mask = intermediate_gate.astype(jnp.float32)
    inner_low = (activated * unit_mask).astype(jnp.bfloat16)
    dense_terms = jnp.dot(inner_low, down_low, preferred_element_type=jnp.float32)
    dense_out = lax.psum(dense_terms, "col") + down_bias
    second_sum = normed_one + dense_rows * hidden_mask * dense_out
    layer_full, second_normed, second_inverse = norm_forward(second_sum, second_gain, second_shift)
    layer_out = lax.dynamic_slice_in_dim(layer_full, col_index * part_width, part_width, 1)
    grad_full = lax.all_gather(cotangent, "col", axis=1, tiled=True).astype(jnp.float32)
    grad_gain_two = jnp.sum(grad_full * second_normed, axis=0)
    grad_shift_two = jnp.sum(grad_full, axis=0)
    grad_second = norm_backward(grad_full, second_normed, second_inverse, second_gain)
    grad_dense_low = (dense_rows * hidden_mask * grad_second).astype(jnp.bfloat16)
    dense_product = dense_out * grad_second
    grad_dense_gate = jnp.sum(
        dense_product.reshape(seq_count, length, model_width) * hidden_mask, axis=(1, 2)
    )
    hidden_from_dense = jnp.sum(dense_rows * dense_product, axis=0)
    grad_down_bias = jnp.sum(grad_dense_low.astype(jnp.float32), axis=0)
    up_low, down_low = (
        lax.all_gather(up_weight.astype(jnp.bfloat16), ("dp", "row"), axis=0, tiled=True),
        lax.all_gather(down_weight.astype(jnp.bfloat16), ("dp", "row"), axis=1, tiled=True),
    )
    grad_down = jnp.einsum(
        "tf,td->fd", inner_low, grad_dense_low, preferred_element_type=jnp.float32
    )
    grad_inner_low = jnp.einsum(
        "td,fd->tf", grad_dense_low, down_low, preferred_element_type=jnp.float32
    ).astype(jnp.bfloat16)
    grad_inner = grad_inner_low.astype(jnp.float32)
    grad_unit_gate = jnp.sum(activated * grad_inner, axis=0)
    (grad_pre,) = gelu_pull(unit_mask * grad_inner)
    grad_pre_low = grad_pre.astype(jnp.bfloat16)
    grad_up_bias = jnp.sum(grad_pre_low.astype(jnp.float32), axis=0)
    grad_up = jnp.einsum("td,tf->df", normed_low, grad_pre_low, preferred_element_type=jnp.float32)
    dense_parts = (
        lax.psum_scatter(grad_up, ("dp", "row"), scatter_dimension=0, tiled=True),
        lax.psum_scatter(grad_down, ("dp", "row"), scatter_dimension=1, tiled=True),
    )
    hidden_terms = jnp.einsum("tf,df->td", grad_pre_low, up_low, preferred_element_type=jnp.float32)
    grad_normed = grad_second + lax.psum(hidden_terms, "col")
    grad_gain_one = jnp.sum(grad_normed * first_normed, axis=0)
    grad_shift_one = jnp.sum(grad_normed, axis=0)
    grad_first = norm_backward(grad_normed, first_normed, first_inverse, first_gain)
    grad_attn_low = (attn_rows * hidden_mask * grad_first).astype(jnp.bfloat16)
    attn_product = attn_out * grad_first
    grad_attn_gate = jnp.sum(
        attn_product.reshape(seq_count, length, model_width) * hidden_mask, axis=(1, 2)
    )
    grad_hidden = hidden_from_dense + jnp.sum(attn_rows * attn_product, axis=0)
    grad_out_bias = jnp.sum(grad_attn_low.astype(jnp.float32), axis=0)
    qkv_low, out_low = (
        lax.all_gather(qkv_weight.astype(jnp.bfloat16), ("dp", "row"), axis=1, tiled=True),
        lax.all_gather(out_weight.astype(jnp.bfloat16), ("dp", "row"), axis=1, tiled=True),
    )
    grad_out = jnp.einsum("tc,td->cd", gated_low, grad_attn_low, preferred_element_type=jnp.float32)
    grad_gated_low = jnp.einsum(
        "td,cd->tc", grad_attn_low, out_low, preferred_element_type=jnp.float32
    ).astype(jnp.bfloat16)
    grad_head_cols = jnp.sum(context * grad_gated_low.astype(jnp.float32), axis=0)
    grad_head = jnp.sum(grad_head_cols.reshape(local_heads, head_size), axis=1)
    grad_context = grad_gated_low * gate_columns.astype(jnp.bfloat16)

    def backward_seq(element):
        query_seq, key_seq, value_seq, grad_seq, log_seq, prefix_value = element
        return attend_back(
            query_seq, key_seq, value_seq, grad_seq, log_seq, prefix_value, block_rows, scale_factor
        )

    grad_query, grad_keys, grad_values = lax.map(
        backward_seq,
        (
            split_heads(query_low),
            split_heads(key_low),
            split_heads(value_low),
            split_heads(grad_context),
            log_totals,
            prefix_length,
        ),
    )
    grad_qkv_low = jnp.stack([grad_query, grad_keys, grad_values]).reshape(3, row_count, head_width)
    grad_qkv_low = grad_qkv_low.astype(jnp.bfloat16)
    grad_query_bias = jnp.sum(grad_qkv_low[0].astype(jnp.float32), axis=0)
    grad_value_bias = jnp.sum(grad_qkv_low[2].astype(jnp.float32), axis=0)
    grad_qkv = jnp.einsum(
        "td,ktf->kdf", token_full, grad_qkv_low, preferred_element_type=jnp.float32
    )
    input_terms = jnp.einsum(
        "ktf,kdf->td", grad_qkv_low, qkv_low, preferred_element_type=jnp.float32
    )
    grad_tokens = lax.psum_scatter(
        input_terms.astype(jnp.bfloat16), "col", scatter_dimension=1, tiled=True
    ).astype(jnp.float32)
    grad_tokens = grad_tokens + lax.dynamic_slice_in_dim(
        grad_first, col_index * part_width, part_width, 1
    )
    grad_up_part, grad_down_part = dense_parts
    grad_qkv_part, grad_out_part = (
        lax.psum_scatter(grad_qkv, ("dp", "row"), scatter_dimension=1, tiled=True),
        lax.psum_scatter(grad_out, ("dp", "row"), scatter_dimension=1, tiled=True),
    )
    seq_total = seq_count * lax.axis_size(("dp", "row"))
    seq_start = lax.axis_index(("dp", "row")) * seq_count
    seq_stack = lax.dynamic_update_slice_in_dim(
        jnp.zeros((2, seq_total), jnp.float32),
        jnp.stack([grad_attn_gate, grad_dense_gate]),
        seq_start,
        1,
    )
    full_stack = jnp.stack(
        [
            grad_out_bias,
            grad_down_bias,
            grad_gain_one,
            grad_shift_one,
            grad_gain_two,
            grad_shift_two,
            grad_hidden,
        ]
    )
    half_stack = jnp.stack([grad_query_bias, grad_value_bias])
    unit_stack = jnp.stack([grad_up_bias, grad_unit_gate])
    full_sum, half_sum, unit_sum, head_sum, seq_sum = lax.psum(
        (full_stack, half_stack, unit_stack, grad_head, seq_stack), ("dp", "row")
    )
    return (
        layer_out,
        grad_tokens,
        grad_qkv_part,
        grad_out_part,
        grad_up_part,
        grad_down_part,
        half_sum[0],
        half_sum[1],
        full_sum[0],
        unit_sum[0],
        full_sum[1],
        full_sum[2],
        full_sum[3],
        full_sum[4],
        full_sum[5],
        head_sum,
        full_sum[6],
        unit_sum[1],
        seq_sum[0],
        seq_sum[1],
    )


low_type = jnp.bfloat16
wide = jnp.float32
mesh_ids = pl.DeviceIdType.MESH


def dot_nn(left, right):
    return jnp.dot(left, right, preferred_element_type=wide)


def dot_nt(left, right):
    return lax.dot_general(left, right, (((1,), (1,)), ((), ())), preferred_element_type=wide)


def rows_at(index, count):
    return pl.ds(pl.multiple_of(index * count, count), count)


def fold_rows(values):
    return jnp.sum(values.reshape(values.shape[0] // 8, 8, values.shape[1]), axis=0)


def norm_parts(values):
    centre = jnp.mean(values, axis=1, keepdims=True)
    centred = values - centre
    spread = jnp.mean(centred * centred, axis=1, keepdims=True)
    inverse = lax.rsqrt(spread + norm_eps)
    return centred * inverse, inverse


class Place:
    def __init__(self, row_size):
        self.dp, self.row, self.col = (lax.axis_index(name) for name in ("dp", "row", "col"))
        self.row_size = row_size
        self.x, self.y = lax.rem(self.dp, 2), self.dp // 2
        self.x_dp = self.y * 2 + (1 - self.x)
        self.y_dp = (1 - self.y) * 2 + self.x

    def x_mate(self):
        return {"dp": self.x_dp}

    def y_mate(self):
        return {"dp": self.y_dp}

    def row_mate(self, step):
        return {"row": lax.rem(self.row + step, self.row_size)}

    def col_mate(self):
        return {"col": 1 - self.col}

    def barrier(self):
        semaphore = pltpu.get_barrier_semaphore()
        mates = [self.x_mate(), self.y_mate(), self.col_mate()]
        mates += [self.row_mate(step) for step in range(1, self.row_size)]
        for mate in mates:
            pl.semaphore_signal(semaphore, inc=1, device_id=mate, device_id_type=mesh_ids)
        pl.semaphore_wait(semaphore, len(mates))


def send(source, target, semaphores, index, mate):
    sent, received = semaphores
    return pltpu.make_async_remote_copy(
        src_ref=source,
        dst_ref=target,
        send_sem=sent.at[index],
        recv_sem=received.at[index],
        device_id=mate,
        device_id_type=mesh_ids,
    )


class Gather:
    def __init__(self, place, shards, chunks, order, own_sem, z_sems, two_sems, three_sems):
        self.place, self.shards, self.chunks = place, shards, chunks
        self.own_sem, self.z_sems, self.two_sems, self.three_sems = own_sem, z_sems, two_sems, three_sems
        self.part = shards[0].shape[0]
        self.block = self.part * place.row_size
        self.half = self.block // 2
        self.steps, self.done = order, 0

    def half_rows(self, dp, half):
        return pl.ds(pl.multiple_of(dp * self.block + half * self.half, 16), self.half)

    def own_rows(self):
        place = self.place
        return pl.ds(pl.multiple_of(place.dp * self.block + place.row * self.part, 16), self.part)

    def own(self, c):
        return pltpu.make_async_copy(self.shards[c], self.chunks[c].at[self.own_rows()], self.own_sem.at[c])

    def along_z(self, c):
        place = self.place
        return [
            send(
                self.shards[c], self.chunks[c].at[self.own_rows()], self.z_sems, (c, step - 1), place.row_mate(step)
            )
            for step in range(1, place.row_size)
        ]

    def pass_on(self, c, dp, half, sems, index, mate):
        at = self.chunks[c].at[self.half_rows(dp, half)]
        return send(at, at, sems, (c, index), mate)

    def second(self, c):
        place = self.place
        return [
            self.pass_on(c, place.dp, 0, self.two_sems, 0, place.x_mate()),
            self.pass_on(c, place.dp, 1, self.two_sems, 1, place.y_mate()),
        ]

    def third(self, c):
        place = self.place
        return [
            self.pass_on(c, place.dp, 0, self.three_sems, 0, place.y_mate()),
            self.pass_on(c, place.dp, 1, self.three_sems, 2, place.x_mate()),
            self.pass_on(c, place.x_dp, 0, self.three_sems, 1, place.y_mate()),
            self.pass_on(c, place.y_dp, 1, self.three_sems, 3, place.x_mate()),
        ]

    def start(self, c):
        self.own(c).start()
        for copy in self.along_z(c):
            copy.start()

    def step(self):
        stage, c = self.steps[self.done]
        self.done += 1
        if stage == 0:
            self.own(c).wait()
            for copy in self.along_z(c):
                copy.wait_recv()
            for copy in self.second(c):
                copy.start()
        elif stage == 1:
            for copy in self.second(c):
                copy.wait_recv()
            for copy in self.third(c):
                copy.start()
        else:
            for copy in self.third(c):
                copy.wait_recv()

    def advance(self, count):
        for _ in range(count):
            if self.done < len(self.steps):
                self.step()

    def need(self, c):
        while self.done <= self.steps.index((2, c)):
            self.step()

    def finish(self):
        self.advance(len(self.steps))
        for c in range(len(self.chunks)):
            for copy in self.along_z(c) + self.second(c) + self.third(c):
                copy.wait_send()


class Scatter:
    def __init__(self, place, chunks, outs, order, first, mid_send, mid, last_send, last, one_sems, two_sems, z_sems):
        self.place, self.chunks, self.outs = place, chunks, outs
        self.first, self.mid_send, self.mid, self.last_send, self.last = first, mid_send, mid, last_send, last
        self.one_sems, self.two_sems, self.z_sems = one_sems, two_sems, z_sems
        self.part = outs[0].shape[0]
        self.block = self.part * place.row_size
        self.half = self.block // 2
        self.count = len(chunks)
        self.steps, self.done, self.begun = order, 0, []

    def half_rows(self, dp, half):
        return pl.ds(pl.multiple_of(dp * self.block + half * self.half, 16), self.half)

    def one(self, c):
        place, chunk, first = self.place, self.chunks[c], self.first[c]
        found = []
        for i in range(2):
            rows = self.half_rows((1 - place.y) * 2 + i, 0)
            found.append(send(chunk.at[rows], first.at[0, i], self.one_sems, (c, i), place.y_mate()))
            rows = self.half_rows(i * 2 + (1 - place.x), 1)
            found.append(send(chunk.at[rows], first.at[1, i], self.one_sems, (c, 2 + i), place.x_mate()))
        return found

    def two(self, c):
        place, mid_send, mid = self.place, self.mid_send[c], self.mid[c]
        return [
            send(mid_send.at[0], mid.at[0], self.two_sems, (c, 0), place.x_mate()),
            send(mid_send.at[1], mid.at[1], self.two_sems, (c, 1), place.y_mate()),
        ]

    def along_z(self, c):
        place = self.place
        found = []
        for step in range(1, place.row_size):
            mate = lax.rem(place.row + step, place.row_size)
            rows = pl.ds(pl.multiple_of(mate * self.part, 16), self.part)
            found.append(
                send(
                    self.last_send[c].at[rows], self.last[c].at[step - 1], self.z_sems, (c, step - 1),
                    place.row_mate(step),
                )
            )
        return found

    def begin(self, c):
        self.begun.append(c)
        for copy in self.one(c):
            copy.start()

    def step(self):
        stage, c = self.steps[self.done]
        self.done += 1
        place, chunk = self.place, self.chunks[c]
        first, mid_send, mid = self.first[c], self.mid_send[c], self.mid[c]
        last_send, last = self.last_send[c], self.last[c]
        if stage == 0:
            for copy in self.one(c):
                copy.wait_recv()
            mid_send[0] = (
                chunk[self.half_rows(place.x_dp, 0), :].astype(wide) + first[0, 1 - place.x].astype(wide)
            ).astype(low_type)
            mid_send[1] = (
                chunk[self.half_rows(place.y_dp, 1), :].astype(wide) + first[1, 1 - place.y].astype(wide)
            ).astype(low_type)
            for copy in self.two(c):
                copy.start()
        elif stage == 1:
            for copy in self.two(c):
                copy.wait_recv()
            for half, slot in ((0, place.x), (1, place.y)):
                last_send[pl.ds(half * self.half, self.half), :] = (
                    chunk[self.half_rows(place.dp, half), :].astype(wide)
                    + first[half, slot].astype(wide)
                    + mid[half].astype(wide)
                ).astype(low_type)
            for copy in self.along_z(c):
                copy.start()
        else:
            total = last_send[pl.ds(pl.multiple_of(place.row * self.part, 16), self.part), :].astype(wide)
            for step, copy in enumerate(self.along_z(c)):
                copy.wait_recv()
                total = total + last[step].astype(wide)
            self.outs[c][...] = total

    def advance(self, count):
        for _ in range(count):
            if self.done < len(self.steps) and self.steps[self.done][1] in self.begun:
                self.step()

    def finish(self):
        self.advance(len(self.steps))
        for c in range(self.count):
            for copy in self.one(c) + self.two(c) + self.along_z(c):
                copy.wait_send()


def masked_tile(tile, query_start, key_start, prefix):
    key_index = key_start + lax.broadcasted_iota(jnp.int32, tile.shape, 0)
    query_index = query_start + lax.broadcasted_iota(jnp.int32, tile.shape, 1)
    return jnp.where((key_index < prefix) | (key_index <= query_index), tile, masked_value)


def key_tiles(block, rows, prefix_most):
    count = max((block + 1) * rows, prefix_most) // rows
    return [(tile, tile >= block) for tile in range(count)]


def flat_row(ref):
    return ref[...].reshape(1, ref.shape[0])


def gate_row(gates, heads, size):
    head = lax.broadcasted_iota(jnp.int32, (1, heads * size), 1) // size
    row = jnp.zeros((1, heads * size), wide)
    for h in range(heads):
        row = jnp.where(head == h, gates[h].astype(wide), row)
    return row


def forward_kernel(
    cut,
    token_part, cot_part, qkv_w, out_w, up_w, down_w, query_bias, value_bias, out_bias, up_bias, down_bias,
    first_gain, first_shift, second_gain, second_shift, hidden_gate, unit_gate,
    head_gate, attention_gate, feedforward_gate, prefix_length,
    wa_out, wm_out, token_out, token_t_out, qkv_out, lse_out, ctx_out, attn_out_out, normed_t_out,
    gelu_out, slope_out, layer_out, second_out, dense_out_low, dense_t_out, sums_out,
    wa, wm, token, token_t, qkv, lse, ctx, attn_out, normed_t, gelu, slope, layer, second, dense_low, dense_t, sums,
    cot, value_t, ctx_t, normed, normed_low, total, precv, drecv, shards_a, shards_m,
    own_sem, z_s, z_r, two_s, two_r, three_s, three_r, col_s, col_r, half_sem, out_sem,
):
    length, heads, size = cut.length, cut.heads, cut.size
    part, rows, fine = cut.part_width, cut.rows, cut.fine
    blocks = length // rows
    pair = 2 * size
    pairs = heads // 2
    group = wm.shape[2]
    place = Place(cut.row_size)
    for p in range(pairs):
        for k in range(3):
            shards_a[p, :, k * pair : (k + 1) * pair] = qkv_w[k, :, p * pair : (p + 1) * pair].astype(low_type)
    shards_a[pairs] = out_w[...].astype(low_type)
    for j in range(2):
        shards_m[2 * j] = up_w[:, j * group : (j + 1) * group].astype(low_type)
        shards_m[2 * j + 1] = down_w[:, j * group : (j + 1) * group].astype(low_type)
    place.barrier()
    prefix = prefix_length[0]
    attn_gate, dense_gate = attention_gate[0].astype(wide), feedforward_gate[0].astype(wide)
    hidden = flat_row(hidden_gate).astype(wide)
    query_bias, value_bias, up_bias, out_bias, down_bias, first_gain, first_shift, second_gain, second_shift = (
        flat_row(ref)
        for ref in (
            query_bias, value_bias, up_bias, out_bias, down_bias, first_gain, first_shift, second_gain, second_shift
        )
    )
    unit_row = flat_row(unit_gate).astype(wide)
    mate = place.col_mate()
    chunks = [wa.at[i] for i in range(pairs + 1)] + [wm.at[i] for i in range(4)]
    shards = [shards_a.at[i] for i in range(pairs + 1)] + [shards_m.at[i] for i in range(4)]
    order = gather_order(len(chunks))
    gather = Gather(place, shards, chunks, order, own_sem, (z_s, z_r), (two_s, two_r), (three_s, three_r))
    own_cols = pl.ds(pl.multiple_of(place.col * part, 128), part)
    halves, crossed = [], []
    for i, (source, target) in enumerate(((token_part, token), (cot_part, cot))):
        halves.append(pltpu.make_async_copy(source, target.at[:, own_cols], half_sem.at[i]))
        crossed.append(send(source, target.at[:, own_cols], (col_s, col_r), i, mate))
    gather.start(0)
    for i in range(2):
        halves[i].start()
        crossed[i].start()
    for c in range(1, len(chunks)):
        gather.start(c)
    outs = []

    def put(source, target):
        copy = pltpu.make_async_copy(source, target, out_sem.at[len(outs)])
        copy.start()
        outs.append(copy)

    sums[...] = jnp.zeros_like(sums)
    halves[0].wait()
    crossed[0].wait_recv()

    @pl.loop(0, blocks)
    def _(b):
        at = rows_at(b, rows)
        token_t[:, at] = token[at, :].T

    put(token, token_out)
    put(token_t, token_t_out)
    lane_head = lax.broadcasted_iota(jnp.int32, (1, pair), 1) // size
    for p in range(pairs):
        gather.need(p)
        query_row = query_bias[:, p * pair : (p + 1) * pair]
        bias = jnp.concatenate(
            [query_row, jnp.zeros_like(query_row), value_bias[:, p * pair : (p + 1) * pair]], axis=1
        )

        @pl.loop(0, blocks)
        def _(b, p=p, bias=bias):
            at = rows_at(b, rows)
            made = dot_nn(token[at, :], wa[p]) + bias
            qkv[p, at, :] = made.astype(low_type)
            value_t[:, at] = made[:, 2 * pair :].T.astype(low_type)

        gather.advance(1)

        @pl.loop(0, 2)
        def _(h, p=p):
            own = jnp.where(lane_head == h, size ** (-0.5), 0.0).astype(low_type)
            head_rows = rows_at(h, size)
            for b in range(blocks):
                query = qkv[p, b * rows : (b + 1) * rows, :pair] * own
                tiles, masked = [], key_tiles(b, rows, cut.prefix_most)
                for tile, needs in masked:
                    score = dot_nt(qkv[p, tile * rows : (tile + 1) * rows, pair : 2 * pair], query)
                    tiles.append(masked_tile(score, b * rows, tile * rows, prefix) if needs else score)
                peak = tiles[0].max(axis=0, keepdims=True)
                for score in tiles[1:]:
                    peak = jnp.maximum(peak, score.max(axis=0, keepdims=True))
                row_total = jnp.zeros_like(peak)
                weights = []
                for score in tiles:
                    weights.append(jnp.exp(score - peak))
                    row_total = row_total + weights[-1].sum(axis=0, keepdims=True)
                share = 1.0 / row_total
                found = jnp.zeros((size, rows), wide)
                for (tile, _), weight in zip(masked, weights):
                    found = found + dot_nn(
                        value_t[head_rows, tile * rows : (tile + 1) * rows], (weight * share).astype(low_type)
                    )
                ctx_t[head_rows, b * rows : (b + 1) * rows] = found
                lse[2 * p + h, :, b * rows : (b + 1) * rows] = peak + jnp.log(row_total)
                if b % 2:
                    for now in range(2):

                        @pl.when(h == now)
                        def _():
                            gather.advance(1)

        @pl.loop(0, blocks)
        def _(b, p=p):
            at = rows_at(b, rows)
            ctx[at, p * pair : (p + 1) * pair] = ctx_t[:, at].T.astype(low_type)

    put(qkv, qkv_out)
    put(lse, lse_out)
    put(ctx, ctx_out)
    gather.need(pairs)
    put(wa, wa_out)
    gate_columns = gate_row(head_gate, heads, size).astype(low_type)

    def swap(source, target, start, b):
        at = pl.ds(b * rows, rows) if isinstance(b, int) else rows_at(b, rows)
        return send(source.at[at], target.at[at], (col_s, col_r), start + b, mate)

    @pl.loop(0, blocks)
    def _(b):
        at = rows_at(b, rows)
        attn_out[at, :] = dot_nt(ctx[at, :] * gate_columns, wa[pairs])
        swap(attn_out, precv, 2, b).start()

    gather.advance(1)
    for b in range(blocks):
        swap(attn_out, precv, 2, b).wait()

        @pl.loop(b * rows // fine, (b + 1) * rows // fine)
        def _(i):
            at = rows_at(i, fine)
            attn = attn_out[at, :] + precv[at, :] + out_bias
            attn_out[at, :] = attn
            first, _ = norm_parts(token[at, :].astype(wide) + attn_gate * hidden * attn)
            out = first * first_gain + first_shift
            normed[at, :] = out
            normed_low[at, :] = out.astype(low_type)

    put(attn_out, attn_out_out)
    gather.advance(1)
    for j in range(2):
        gather.need(pairs + 1 + 2 * j)
        bias_row = up_bias[:, j * group : (j + 1) * group]
        unit_mask = unit_row[:, j * group : (j + 1) * group].astype(low_type)

        @pl.loop(0, blocks)
        def _(b, j=j, bias_row=bias_row):
            at = rows_at(b, rows)
            pre = dot_nn(normed_low[at, :], wm[2 * j]) + bias_row
            share = 0.5 * (1.0 + lax.erf(pre * (2.0 ** -0.5)))
            gelu[j, at, :] = (pre * share).astype(low_type)
            density = jnp.exp(-0.5 * pre * pre) * ((2.0 * math.pi) ** -0.5)
            slope[j, at, :] = (share + pre * density).astype(low_type)
            if j == 0:
                normed_t[:, at] = normed_low[at, :].T

        gather.need(pairs + 2 + 2 * j)

        @pl.loop(0, blocks)
        def _(b, j=j, unit_mask=unit_mask):
            at = rows_at(b, rows)
            made = dot_nt(gelu[j, at, :] * unit_mask, wm[2 * j + 1])
            if j == 0:
                total[at, :] = made
            else:
                total[at, :] += made
                swap(total, drecv, 2 + blocks, b).start()

    put(normed_t, normed_t_out)
    put(gelu, gelu_out)
    put(slope, slope_out)
    put(wm, wm_out)
    halves[1].wait()
    crossed[1].wait_recv()
    for b in range(blocks):
        swap(total, drecv, 2 + blocks, b).wait_recv()

        @pl.loop(b * rows // fine, (b + 1) * rows // fine)
        def _(i):
            at = rows_at(i, fine)
            dense = total[at, :] + drecv[at, :] + down_bias
            last, inverse = norm_parts(normed[at, :] + dense_gate * hidden * dense)
            full = last * second_gain + second_shift
            layer[at, :] = jnp.where(place.col == 0, full[:, :part], full[:, part:])
            grad = cot[at, :].astype(wide)
            scaled = grad * second_gain
            one = jnp.mean(scaled, axis=1, keepdims=True)
            two = jnp.mean(scaled * last, axis=1, keepdims=True)
            made = inverse * (scaled - one - last * two)
            second[at, :] = made
            gated = (dense_gate * hidden * made).astype(low_type)
            dense_low[at, :] = gated
            product = dense * made
            sums[0] += fold_rows(grad * last)
            sums[1] += fold_rows(grad)
            sums[2] += fold_rows(gated.astype(wide))
            sums[3] += fold_rows(product)

        at = pl.ds(b * rows, rows)
        dense_t[:, at] = dense_low[at, :].T

    put(layer, layer_out)
    put(second, second_out)
    put(dense_low, dense_out_low)
    put(dense_t, dense_t_out)
    put(sums, sums_out)
    gather.finish()
    for copy in crossed:
        copy.wait_send()
    for b in range(blocks):
        swap(total, drecv, 2 + blocks, b).wait_send()
    for copy in outs:
        copy.wait()


def backward_kernel(
    cut,
    wa_in, wm_in, token_in, token_t_in, qkv_in, lse_in, ctx_in, attn_out_in, normed_t_in,
    gelu_in, slope_in, second_in, dense_low_in, dense_t_in, sums_in,
    first_gain, hidden_gate, unit_gate, head_gate, attention_gate, feedforward_gate, prefix_length,
    grad_token, small_out, *rest,
):
    length, width, heads, size = cut.length, cut.width, cut.heads, cut.size
    part, rows, fine = cut.part_width, cut.rows, cut.fine
    blocks = length // rows
    pair = 2 * size
    pairs = heads // 2
    count = pairs + 5
    rest = list(rest)

    def take(number):
        taken = rest[:number]
        del rest[:number]
        return taken

    grads = take(count)
    (wa, wm, token, token_t, qkv, lse, ctx, attn_out, normed_t, gelu, slope, second, dense_low, dense_t, sums) = take(15)
    (total, precv, fsend, frecv, ctx_grad, triple, key_grad, value_grad, query_t, key_t) = take(10)
    (small, small_x, small_y, small_z, unit_sums, head_sums) = take(6)
    buffers, first, mid_send, mid, last_send, last = (take(count) for _ in range(6))
    (in_sem, one_s, one_r, two_s, two_r, z_s, z_r, col_s, col_r, small_s, small_r) = take(11)
    place = Place(cut.row_size)
    loads = {}
    for i, (name, source, target) in enumerate(
        (
            ("dense_t", dense_t_in, dense_t),
            ("gelu", gelu_in, gelu),
            ("dense_low", dense_low_in, dense_low),
            ("wm", wm_in, wm),
            ("slope", slope_in, slope),
            ("normed_t", normed_t_in, normed_t),
            ("sums", sums_in, sums),
            ("second", second_in, second),
            ("attn_out", attn_out_in, attn_out),
            ("token", token_in, token),
            ("wa", wa_in, wa),
            ("ctx", ctx_in, ctx),
            ("qkv", qkv_in, qkv),
            ("lse", lse_in, lse),
            ("token_t", token_t_in, token_t),
        )
    ):
        loads[name] = pltpu.make_async_copy(source, target, in_sem.at[i])
        loads[name].start()

    def load(*names):
        for name in names:
            loads[name].wait()

    place.barrier()
    prefix = prefix_length[0]
    attn_gate, dense_gate = attention_gate[0].astype(wide), feedforward_gate[0].astype(wide)
    hidden, unit_row = flat_row(hidden_gate).astype(wide), flat_row(unit_gate).astype(wide)
    first_gain = flat_row(first_gain)
    mate = place.col_mate()
    scatter = Scatter(
        place, buffers, grads, scatter_order(pairs), first, mid_send, mid, last_send, last,
        (one_s, one_r), (two_s, two_r), (z_s, z_r),
    )
    unit_sums[...] = jnp.zeros_like(unit_sums)
    head_sums[...] = jnp.zeros_like(head_sums)
    group = wm.shape[2]

    def swap(source, target, start, b):
        at = pl.ds(b * rows, rows) if isinstance(b, int) else rows_at(b, rows)
        return send(source.at[at], target.at[at], (col_s, col_r), start + b, mate)

    def product(target, left, right, mask=None):
        @pl.loop(0, width // rows)
        def _(i):
            at = rows_at(i, rows)
            made = dot_nn(left[at, :], right[...])
            target[at, :] = (made if mask is None else made * mask).astype(low_type)

    masks = [unit_row[:, j * group : (j + 1) * group] for j in range(2)]
    load("dense_t", "gelu")
    for j in range(2):
        product(buffers[j], dense_t, gelu.at[j], masks[j])
        scatter.begin(j)
    load("dense_low", "wm", "slope")
    for j in range(2):

        @pl.loop(0, blocks)
        def _(b, j=j):
            at = rows_at(b, rows)
            inner = dot_nn(dense_low[at, :], wm[2 * j + 1]).astype(low_type).astype(wide)
            unit_sums[2 + j] += fold_rows(gelu[j, at, :].astype(wide) * inner)
            pre = (masks[j] * inner * slope[j, at, :].astype(wide)).astype(low_type)
            slope[j, at, :] = pre
            unit_sums[j] += fold_rows(pre.astype(wide))
            made = dot_nt(pre, wm[2 * j])
            if j == 0:
                total[at, :] = made
            else:
                total[at, :] += made
                swap(total, precv, 0, b).start()

        scatter.advance(1)
        if j == 0:
            load("normed_t")
        product(buffers[2 + j], normed_t, slope.at[j])
        scatter.begin(2 + j)

    load("sums", "second", "attn_out", "token")
    for b in range(blocks):
        swap(total, precv, 0, b).wait_recv()

        @pl.loop(b * rows // fine, (b + 1) * rows // fine)
        def _(i):
            at = rows_at(i, fine)
            attn = attn_out[at, :]
            gate_cols = attn_gate * hidden
            normed, inverse = norm_parts(token[at, :].astype(wide) + gate_cols * attn)
            grad = second[at, :] + (total[at, :] + precv[at, :])
            scaled = grad * first_gain
            one = jnp.mean(scaled, axis=1, keepdims=True)
            two = jnp.mean(scaled * normed, axis=1, keepdims=True)
            made = inverse * (scaled - one - normed * two)
            second[at, :] = made
            gated = (gate_cols * made).astype(low_type)
            dense_low[at, :] = gated
            sums[4] += fold_rows(grad * normed)
            sums[5] += fold_rows(grad)
            sums[6] += fold_rows(gated.astype(wide))
            sums[7] += fold_rows(attn * made)

        at = pl.ds(b * rows, rows)
        dense_t[:, at] = dense_low[at, :].T
        if b % 2:
            scatter.advance(1)

    for b in range(blocks):
        swap(total, precv, 0, b).wait_send()
    load("wa", "ctx", "qkv", "lse", "token_t")
    gate_columns = gate_row(head_gate, heads, size)

    @pl.loop(0, blocks)
    def _(b):
        at = rows_at(b, rows)
        gated = dot_nn(dense_low[at, :], wa[pairs]).astype(low_type).astype(wide)
        seen = ctx[at, :].astype(wide)
        head_sums[...] += fold_rows(seen * gated)
        ctx_grad[at, :] = (gated * gate_columns).astype(low_type)
        ctx[at, :] = (seen * gate_columns).astype(low_type)

    product(buffers[4], dense_t, ctx)
    scatter.begin(4)
    scatter.advance(1)
    lane_head = lax.broadcasted_iota(jnp.int32, (1, pair), 1) // size
    bias_sums = []
    for p in range(pairs):

        @pl.loop(0, blocks)
        def _(b, p=p):
            at = rows_at(b, rows)
            key_t[:, at] = qkv[p, at, pair : 2 * pair].astype(wide).T.astype(low_type)

        key_grad[...] = jnp.zeros_like(key_grad)
        value_grad[...] = jnp.zeros_like(value_grad)

        @pl.loop(0, 2)
        def _(h, p=p):
            own = jnp.where(lane_head == h, size ** (-0.5), 0.0).astype(low_type)
            one_head = jnp.where(lane_head == h, 1.0, 0.0).astype(low_type)
            head_rows = rows_at(h, size)
            for b in range(blocks):
                query = qkv[p, b * rows : (b + 1) * rows, :pair] * own
                context = ctx_grad[b * rows : (b + 1) * rows, p * pair : (p + 1) * pair] * one_head
                logs = lse[2 * p + h, :, b * rows : (b + 1) * rows]
                inner = jnp.zeros_like(logs)
                kept, masked = [], key_tiles(b, rows, cut.prefix_most)
                for tile, needs in masked:
                    score = dot_nt(qkv[p, tile * rows : (tile + 1) * rows, pair : 2 * pair], query)
                    score = masked_tile(score, b * rows, tile * rows, prefix) if needs else score
                    prob = jnp.exp(score - logs)
                    grad_prob = dot_nt(qkv[p, tile * rows : (tile + 1) * rows, 2 * pair :], context)
                    inner = inner + (prob * grad_prob).sum(axis=0, keepdims=True)
                    kept.append((prob, grad_prob))
                found = jnp.zeros((size, rows), wide)
                for (tile, _), (prob, grad_prob) in zip(masked, kept):
                    at = slice(tile * rows, (tile + 1) * rows)
                    grad_score = (prob * (grad_prob - inner)).astype(low_type)
                    value_grad[at, :] += dot_nn(prob.astype(low_type), context)
                    key_grad[at, :] += dot_nn(grad_score, query)
                    found = found + dot_nn(key_t[head_rows, at], grad_score)
                query_t[head_rows, b * rows : (b + 1) * rows] = found * size ** (-0.5)
                if b % 2:
                    for now in range(2):

                        @pl.when(h == now)
                        def _():
                            scatter.advance(1)

        query_sum = jnp.zeros((8, pair), wide)
        value_sum = jnp.zeros((8, pair), wide)
        for b in range(blocks):
            at = pl.ds(b * rows, rows)
            query_low = query_t[:, at].T.astype(low_type)
            value_low = value_grad[at, :].astype(low_type)
            triple[at, :pair] = query_low
            triple[at, pair : 2 * pair] = key_grad[at, :].astype(low_type)
            triple[at, 2 * pair :] = value_low
            query_sum += fold_rows(query_low.astype(wide))
            value_sum += fold_rows(value_low.astype(wide))
        bias_sums.append((query_sum, value_sum))
        product(buffers[5 + p], token_t, triple)
        scatter.begin(5 + p)
        if p < pairs - 1:
            scatter.advance(1)

        @pl.loop(0, blocks)
        def _(b, p=p):
            at = rows_at(b, rows)
            made = dot_nt(triple[at, :], wa[p])
            if p > 0:
                made = total[at, :] + made
            if p < pairs - 1:
                total[at, :] = made
            else:
                mine = jnp.where(place.col == 0, made[:, :part], made[:, part:])
                other = jnp.where(place.col == 0, made[:, part:], made[:, :part])
                kept = second[at, :]
                grad_token[at, :] = mine + jnp.where(place.col == 0, kept[:, :part], kept[:, part:])
                fsend[at, :] = other.astype(low_type)
                swap(fsend, frecv, blocks, b).start()

    def whole(values):
        return jnp.sum(values, axis=0, keepdims=True)

    dense_col, attn_col = whole(sums[3]), whole(sums[7])
    seq_lane = lax.broadcasted_iota(jnp.int32, (1, width), 1)
    here = place.dp * place.row_size + place.row
    dense_all = jnp.sum(dense_col * hidden, axis=1, keepdims=True)
    attn_all = jnp.sum(attn_col * hidden, axis=1, keepdims=True)
    seq_row = jnp.where(seq_lane == here, attn_all, 0.0) + jnp.where(seq_lane == here + width // 2, dense_all, 0.0)
    small[0:1, :] = whole(sums[6])
    small[1:2, :] = whole(sums[2])
    small[2:3, :] = whole(sums[4])
    small[3:4, :] = whole(sums[5])
    small[4:5, :] = whole(sums[0])
    small[5:6, :] = whole(sums[1])
    small[6:7, :] = dense_gate * dense_col + attn_gate * attn_col
    small[7:8, :] = seq_row
    for j in range(4):
        small[8 + j : 9 + j, :] = whole(unit_sums[j])
    for p in range(pairs):
        small[12:13, p * pair : (p + 1) * pair] = whole(bias_sums[p][0])
        small[12:13, part + p * pair : part + (p + 1) * pair] = whole(bias_sums[p][1])
    small[13:14, :part] = whole(head_sums[...])
    small[13:14, part:] = jnp.zeros((1, part), wide)
    small[14:16, :] = jnp.zeros((2, width), wide)
    copy_x = send(small, small_x.at[0], (small_s, small_r), 0, place.x_mate())
    copy_x.start()
    scatter.advance(1)
    copy_x.wait_recv()
    small_x[1] = small[...] + small_x[0]
    copy_y = send(small_x.at[1], small_y.at[0], (small_s, small_r), 1, place.y_mate())
    copy_y.start()
    scatter.advance(1)
    copy_y.wait_recv()
    mine = small_x[1] + small_y[0]
    small_y[1] = mine
    small_z[place.row] = mine
    copies = [
        send(small_y.at[1], small_z.at[place.row], (small_s, small_r), 1 + step, place.row_mate(step))
        for step in range(1, cut.row_size)
    ]
    for copy in copies:
        copy.start()
    for b in range(blocks):
        swap(fsend, frecv, blocks, b).wait_recv()
        at = pl.ds(b * rows, rows)
        grad_token[at, :] += frecv[at, :].astype(wide)
    scatter.finish()
    for copy in copies:
        copy.wait_recv()
    result = small_z[0]
    for z in range(1, cut.row_size):
        result = result + small_z[z]
    small_out[...] = result
    for copy in [copy_x, copy_y] + copies:
        copy.wait_send()
    for b in range(blocks):
        swap(fsend, frecv, blocks, b).wait_send()


def place_kernel(
    cut,
    small, down_0, down_1, up_0, up_1, grad_out_t, *rest,
):
    pairs, pair, part, width = cut.heads // 2, 2 * cut.size, cut.part_width, cut.width
    pieces, rest = rest[:pairs], rest[pairs:]
    (
        grad_qkv, grad_out, grad_up, grad_down, query_bias, value_bias, out_bias, up_bias, down_bias, first_gain,
        first_shift, second_gain, second_shift, head, hidden, unit, attention, feedforward,
    ) = rest
    group = cut.units // 2
    for p, piece in enumerate(pieces):
        for k in range(3):
            grad_qkv[k, :, p * pair : (p + 1) * pair] = piece[:, k * pair : (k + 1) * pair]
    grad_out[...] = grad_out_t[...]
    for j, (up, down) in enumerate(((up_0, down_0), (up_1, down_1))):
        grad_up[:, j * group : (j + 1) * group] = up[...]
        grad_down[:, j * group : (j + 1) * group] = down[...]

    def flat(target, values):
        target[...] = values.reshape(target.shape)

    flat(up_bias, jnp.concatenate([small[8:9, :], small[9:10, :]], axis=1))
    flat(unit, jnp.concatenate([small[10:11, :], small[11:12, :]], axis=1))
    flat(query_bias, small[12:13, :part])
    flat(value_bias, small[12:13, part:])
    for row, target in enumerate((out_bias, down_bias, first_gain, first_shift, second_gain, second_shift, hidden)):
        flat(target, small[row : row + 1, :])
    lane = lax.broadcasted_iota(jnp.int32, (1, part), 1) // cut.size
    slot = lax.broadcasted_iota(jnp.int32, (1, cut.heads), 1)
    found = jnp.zeros((1, cut.heads), wide)
    for h in range(cut.heads):
        one = jnp.sum(jnp.where(lane == h, small[13:14, :part], 0.0), axis=1, keepdims=True)
        found = jnp.where(slot == h, one, found)
    flat(head, found)
    seq_total = attention.shape[0]
    flat(attention, small[7:8, :seq_total])
    flat(feedforward, small[7:8, width // 2 : width // 2 + seq_total])


def gather_order(count):
    return [(stage, t - stage) for t in range(count + 2) for stage in range(3) if 0 <= t - stage < count]


def scatter_order(pairs):
    out = [(0, 0), (0, 1), (0, 2), (1, 0), (1, 1), (0, 3), (2, 0), (1, 2), (2, 1), (1, 3), (0, 4), (2, 2), (1, 4), (2, 3)]
    before = 4
    for c in range(5, 5 + pairs):
        out += [(0, c), (2, before), (1, c)]
        before = c
    return out + [(2, before)]


class Cut(NamedTuple):
    length: int
    width: int
    part_width: int
    heads: int
    size: int
    units: int
    part: int
    row_size: int
    rows: int
    fine: int
    prefix_most: int


def any_spec():
    return pl.BlockSpec(memory_space=pl.ANY)


def vmem_spec():
    return pl.BlockSpec(memory_space=pltpu.VMEM)


def smem_spec():
    return pl.BlockSpec(memory_space=pltpu.SMEM)


def like(items):
    return [jax.ShapeDtypeStruct(shape, kind) for shape, kind in items]


def scratch(items):
    return [pltpu.VMEM(shape, kind) for shape, kind in items]


def dma(*shape):
    return pltpu.SemaphoreType.DMA(shape)


vmem_most = 67043328


def run_forward(cut, token_part, cot_part, *args):
    length, width, half = cut.length, cut.width, cut.part_width
    group = cut.units // 2
    chunks_a, chunks = cut.heads // 2 + 1, cut.heads // 2 + 5
    blocks = length // cut.rows
    kept = [
        ((chunks_a, width, half), low_type),
        ((4, width, group), low_type),
        ((length, width), low_type),
        ((width, length), low_type),
        ((cut.heads // 2, length, half), low_type),
        ((cut.heads, 1, length), wide),
        ((length, half), low_type),
        ((length, width), wide),
        ((width, length), low_type),
        ((2, length, group), low_type),
        ((2, length, group), low_type),
        ((length, half), wide),
        ((length, width), wide),
        ((length, width), low_type),
        ((width, length), low_type),
        ((8, 8, width), wide),
    ]
    own = [
        ((length, width), low_type),
        ((2 * cut.size, length), low_type),
        ((2 * cut.size, length), wide),
        ((length, width), wide),
        ((length, width), low_type),
        ((length, width), wide),
        ((length, width), wide),
        ((length, width), wide),
        ((chunks_a, cut.part, half), low_type),
        ((4, cut.part, group), low_type),
    ]
    z = cut.row_size - 1
    semaphores = [dma(chunks), dma(chunks, z), dma(chunks, z), dma(chunks, 2), dma(chunks, 2), dma(chunks, 4), dma(chunks, 4)]
    semaphores += [dma(2 + 2 * blocks), dma(2 + 2 * blocks), dma(2), dma(len(kept))]
    return pl.pallas_call(
        partial(forward_kernel, cut),
        out_shape=like(kept),
        in_specs=[any_spec()] * 2 + [vmem_spec()] * (len(args) - 4) + [smem_spec()] * 4,
        out_specs=[any_spec()] * len(kept),
        scratch_shapes=scratch(kept) + scratch(own) + semaphores,
        compiler_params=pltpu.CompilerParams(collective_id=0, has_side_effects=True, vmem_limit_bytes=vmem_most),
        name="layer_forward",
    )(token_part, cot_part, *args)


def run_backward(cut, kept, *args):
    length, width, half = cut.length, cut.width, cut.part_width
    group = cut.units // 2
    pairs = cut.heads // 2
    blocks = length // cut.rows
    columns = [group] * 4 + [half] * (pairs + 1)
    count = len(columns)
    outs = [((length, half), wide), ((16, width), wide)] + [((cut.part, n), wide) for n in columns]
    loaded = [(item.shape, item.dtype) for item in kept]
    own = [
        ((length, width), wide),
        ((length, width), wide),
        ((length, half), low_type),
        ((length, half), low_type),
        ((length, half), low_type),
        ((length, half), low_type),
        ((length, 2 * cut.size), wide),
        ((length, 2 * cut.size), wide),
        ((2 * cut.size, length), wide),
        ((2 * cut.size, length), low_type),
        ((16, width), wide),
        ((2, 16, width), wide),
        ((2, 16, width), wide),
        ((cut.row_size, 16, width), wide),
        ((4, 8, width), wide),
        ((8, half), wide),
    ]
    quarter = cut.part * cut.row_size // 2
    own += [((width, n), low_type) for n in columns]
    own += [((2, 2, quarter, n), low_type) for n in columns]
    own += [((2, quarter, n), low_type) for n in columns]
    own += [((2, quarter, n), low_type) for n in columns]
    own += [((2 * quarter, n), low_type) for n in columns]
    own += [((cut.row_size - 1, cut.part, n), low_type) for n in columns]
    z = cut.row_size - 1
    semaphores = [dma(len(kept)), dma(count, 4), dma(count, 4), dma(count, 2), dma(count, 2), dma(count, z), dma(count, z)]
    semaphores += [dma(2 * blocks), dma(2 * blocks), dma(2 + z), dma(2 + z)]
    return pl.pallas_call(
        partial(backward_kernel, cut),
        out_shape=like(outs),
        in_specs=[any_spec()] * len(kept) + [vmem_spec()] * 3 + [smem_spec()] * 4,
        out_specs=[vmem_spec()] * len(outs),
        scratch_shapes=scratch(loaded) + scratch(own) + semaphores,
        compiler_params=pltpu.CompilerParams(collective_id=1, has_side_effects=True, vmem_limit_bytes=vmem_most),
        name="layer_backward",
    )(*kept, *args)


def fused_device(
    cut,
    tokens, cotangent, qkv_weight, out_weight, up_weight, down_weight, query_bias, value_bias, out_bias, up_bias,
    down_bias, first_gain, first_shift, second_gain, second_shift, head_gate, hidden_gate, intermediate_gate,
    attention_gate, feedforward_gate, prefix_length,
):
    half, width, units, part = cut.part_width, cut.width, cut.units, cut.part
    rows = [
        query_bias, value_bias, out_bias, up_bias, down_bias, first_gain, first_shift, second_gain, second_shift,
        hidden_gate, intermediate_gate,
    ]
    scalars = [head_gate, attention_gate, feedforward_gate, prefix_length]
    weights = [qkv_weight, out_weight.T, up_weight, down_weight.T]
    kept = list(run_forward(cut, tokens, cotangent, *weights, *rows, *scalars))
    layer_out = kept.pop(11)
    made = run_backward(cut, kept, rows[5], rows[9], rows[10], *scalars)
    grad_tokens, small = made[0], made[1]
    seq_total = lax.axis_size(("dp", "row"))
    lanes = [half, half, width, units, width, width, width, width, width, cut.heads, width, units, seq_total, seq_total]
    shapes = [(3, part, half), (part, half), (part, units), (part, units)] + [(n,) for n in lanes]
    outs = pl.pallas_call(
        partial(place_kernel, cut),
        out_shape=like([(shape, wide) for shape in shapes]),
        in_specs=[vmem_spec()] * (len(made) - 1),
        out_specs=[vmem_spec()] * len(shapes),
        name="place_results",
    )(small, *made[2:])
    return (layer_out, grad_tokens, outs[0], outs[1].T, outs[2], outs[3].T, *outs[4:])


def cut_of(args):
    tokens, qkv_weight, up_weight, head_gate, prefix_length = args[0], args[2], args[4], args[15], args[20]
    length, part_width = tokens.shape
    part, width = qkv_weight.shape[1], args[11].shape[0]
    heads = head_gate.shape[0]
    row_size, dp_size = lax.axis_size("row"), lax.axis_size("dp")
    fits = (
        prefix_length.shape[0] == 1
        and lax.axis_size("col") == 2
        and dp_size == 4
        and row_size % 2 == 0
        and part % 16 == 0
        and heads % 2 == 0
        and part_width == qkv_weight.shape[2]
        and part_width == 3 * (2 * part_width // heads)
        and (2 * part_width // heads) % 128 == 0
        and width % 256 == 0
        and length % 512 == 0
        and up_weight.shape[1] == 2 * width
    )
    if not fits:
        return None
    return Cut(
        length, width, part_width, heads, part_width // heads, up_weight.shape[1], part, row_size, 256, 128, length // 2
    )


def any_device(*args):
    cut = cut_of(args)
    return per_device(*args) if cut is None else fused_device(cut, *args)


def solution(mesh):
    placed = (
        P(("dp", "row"), "col"),
        P(("dp", "row"), "col"),
        P(None, ("dp", "row"), "col"),
        P("col", ("dp", "row")),
        P(("dp", "row"), "col"),
        P("col", ("dp", "row")),
        P("col"),
        P("col"),
        P(),
        P("col"),
        P(),
        P(),
        P(),
        P(),
        P(),
        P("col"),
        P(),
        P("col"),
        P(("dp", "row")),
        P(("dp", "row")),
        P(("dp", "row")),
    )
    return jax.shard_map(
        any_device,
        mesh=mesh,
        in_specs=placed,
        out_specs=(
            P(("dp", "row"), "col"),
            P(("dp", "row"), "col"),
            P(None, ("dp", "row"), "col"),
            P("col", ("dp", "row")),
            P(("dp", "row"), "col"),
            P("col", ("dp", "row")),
            P("col"),
            P("col"),
            P(),
            P("col"),
            P(),
            P(),
            P(),
            P(),
            P(),
            P("col"),
            P(),
            P("col"),
            P(),
            P(),
        ),
        check_vma=False,
    )
```

profile of v0, /device:TPU:0, one launch (start us, length us, event | category | flops | bytes accessed | tf_op | source)
XLA Modules:
  0.0 196.3 jit_solution(9591546728962464321)
XLA Ops:
  2.6 89.4 %layer_forward.1 = (bf16[4,768,384]{2,1,0:T(8,128)(2,1)}, bf16[4,768,768]{2,1,0:T(8,128)(2,1)}, bf16[1024,768]{1,0:T(8,128)(2,1)}, bf16[768,1024]{1,0:T(8,128)(2...) custom-call(bf16[1024,384]{1,0:T(8,128)(2,1)} %token_part.1, ...), custom_call_target="tpu_custom_call" | custom-call | tf_op jit(solution)/shard_map/layer_forward/pallas_call | solution.py:1275
  92.0 98.1 %layer_backward.1 = (f32[1024,384]{1,0:T(8,128)}, f32[16,768]{1,0:T(8,128)}, f32[48,768]{1,0:T(8,128)}, f32[48,768]{1,0:T(8,128)}, f32[48,768]{1,0:T(8,128)}, /*...) custom-call(bf16[4,768,384]{2,1,0:T(8,128)(2,1)} %get-tuple-element.65.wa, ...), custom_call_target="tpu_custom_call" | custom-call | tf_op jit(solution)/shard_map/layer_backward/pallas_call | solution.py:1323
  190.2 2.2 %place_results.1 = (f32[3,48,384]{2,1,0:T(8,128)}, f32[48,384]{1,0:T(8,128)}, f32[48,1536]{1,0:T(8,128)}, f32[48,1536]{1,0:T(8,128)}, f32[384]{0:T(512)}, /*inde...) custom-call(f32[16,768]{1,0:T(8,128)} %get-tuple-element.81.small, ...), custom_call_target="tpu_custom_call" | custom-call | tf_op jit(solution)/shard_map/place_results/pallas_call | solution.py:1354
  192.4 0.0 copy-start
  192.4 2.8 %copy.46 = f32[1024,384]{1,0:T(8,128)} copy(f32[1024,384]{1,0:T(8,128)} %get-tuple-element.128) | data formatting | bytes 3145728
  195.2 0.0 copy-done
  195.2 1.1 copy.47
Async XLA Ops:
  192.4 2.8 %copy-start = (f32[1024,384]{1,0:T(8,128)S(1)}, f32[1024,384]{1,0:T(8,128)}, u32[]{:S(2)}) copy-start(f32[1024,384]{1,0:T(8,128)} %get-tuple-element.129) | copy-start | bytes 4718596
where the time goes:
time: 197 us; the launch traced here: 196 us
  Pallas kernels  190 us (96%)
  local copies, waits for them, and re-layouts  3.92 us (2%)
  between operations  2.63 us (1%)
    pallas_call x1, Pallas kernels, run_backward(): pl.pallas_call(partial(backward_kernel, cut), out_shape=like(outs), in_sp...  98.1 us
    pallas_call x1, Pallas kernels, run_forward(): pl.pallas_call(partial(forward_kernel, cut), out_shape=like(kept), in_spe...  89.4 us

commit v1 on v0

--- a/solution.py
+++ b/solution.py
@@ -616,22 +616,35 @@
     return row
 
 
-def forward_kernel(
+def layer_kernel(
     cut,
     token_part, cot_part, qkv_w, out_w, up_w, down_w, query_bias, value_bias, out_bias, up_bias, down_bias,
     first_gain, first_shift, second_gain, second_shift, hidden_gate, unit_gate,
     head_gate, attention_gate, feedforward_gate, prefix_length,
-    wa_out, wm_out, token_out, token_t_out, qkv_out, lse_out, ctx_out, attn_out_out, normed_t_out,
-    gelu_out, slope_out, layer_out, second_out, dense_out_low, dense_t_out, sums_out,
-    wa, wm, token, token_t, qkv, lse, ctx, attn_out, normed_t, gelu, slope, layer, second, dense_low, dense_t, sums,
-    cot, value_t, ctx_t, normed, normed_low, total, precv, drecv, shards_a, shards_m,
-    own_sem, z_s, z_r, two_s, two_r, three_s, three_r, col_s, col_r, half_sem, out_sem,
+    layer_out, token_out, small_out, *rest,
 ):
-    length, heads, size = cut.length, cut.heads, cut.size
+    length, width, heads, size = cut.length, cut.width, cut.heads, cut.size
     part, rows, fine = cut.part_width, cut.rows, cut.fine
     blocks = length // rows
+    own_count = blocks // 2
     pair = 2 * size
     pairs = heads // 2
+    count = pairs + 5
+    rest = list(rest)
+
+    def take(number):
+        taken = rest[:number]
+        del rest[:number]
+        return taken
+
+    grads = take(count)
+    (wa, wm, token, token_t, qkv, lse, ctx, attn_out, normed_t, gelu, slope, second, low, dense_t, sums) = take(15)
+    (cot, total, arrive_a, arrive_b, stage, token_recv, ctx_grad, triple, key_grad, value_grad) = take(10)
+    (pair_wide, pair_low, shards_a, shards_m) = take(4)
+    (small, small_c, small_x, small_y, small_z, unit_sums, head_sums) = take(7)
+    buffers, first, mid_send, mid, last_send, last = (take(count) for _ in range(6))
+    (own_sem, gz_s, gz_r, g2_s, g2_r, g3_s, g3_r, half_sem, out_sem, s1_s, s1_r, s2_s, s2_r, sz_s, sz_r) = take(15)
+    (col_s, col_r, small_s, small_r) = take(4)
     group = wm.shape[2]
     place = Place(cut.row_size)
     for p in range(pairs):
@@ -644,48 +657,92 @@
     place.barrier()
     prefix = prefix_length[0]
     attn_gate, dense_gate = attention_gate[0].astype(wide), feedforward_gate[0].astype(wide)
-    hidden = flat_row(hidden_gate).astype(wide)
+    hidden, unit_row = flat_row(hidden_gate).astype(wide), flat_row(unit_gate).astype(wide)
     query_bias, value_bias, up_bias, out_bias, down_bias, first_gain, first_shift, second_gain, second_shift = (
         flat_row(ref)
         for ref in (
             query_bias, value_bias, up_bias, out_bias, down_bias, first_gain, first_shift, second_gain, second_shift
         )
     )
-    unit_row = flat_row(unit_gate).astype(wide)
-    mate = place.col_mate()
     chunks = [wa.at[i] for i in range(pairs + 1)] + [wm.at[i] for i in range(4)]
     shards = [shards_a.at[i] for i in range(pairs + 1)] + [shards_m.at[i] for i in range(4)]
-    order = gather_order(len(chunks))
-    gather = Gather(place, shards, chunks, order, own_sem, (z_s, z_r), (two_s, two_r), (three_s, three_r))
+    gather = Gather(
+        place, shards, chunks, gather_order(count), own_sem, (gz_s, gz_r), (g2_s, g2_r), (g3_s, g3_r)
+    )
+    scatter = Scatter(
+        place, buffers, grads, scatter_order(pairs), first, mid_send, mid, last_send, last,
+        (s1_s, s1_r), (s2_s, s2_r), (sz_s, sz_r),
+    )
+
+    def to_mate(source, target, index):
+        return send(source, target, (col_s, col_r), index, place.col_mate())
+
+    def own_block(i):
+        return rows_at(place.col * own_count + i, rows)
+
+    def mate_block(i):
+        return rows_at((1 - place.col) * own_count + i, rows)
+
+    def near(i):
+        return pl.ds(i * rows, rows) if isinstance(i, int) else rows_at(i, rows)
+
+    def mate_first(t):
+        return lax.rem((1 - place.col) * own_count + t, blocks)
+
     own_cols = pl.ds(pl.multiple_of(place.col * part, 128), part)
-    halves, crossed = [], []
-    for i, (source, target) in enumerate(((token_part, token), (cot_part, cot))):
-        halves.append(pltpu.make_async_copy(source, target.at[:, own_cols], half_sem.at[i]))
-        crossed.append(send(source, target.at[:, own_cols], (col_s, col_r), i, mate))
+    own_half = pl.ds(pl.multiple_of(place.col * (length // 2), rows), length // 2)
+    mate_half = pl.ds(pl.multiple_of((1 - place.col) * (length // 2), rows), length // 2)
+    token_own = pltpu.make_async_copy(token_part, token.at[:, own_cols], half_sem.at[0])
+    token_sent = to_mate(token_part, token.at[:, own_cols], 0)
+    cot_own = pltpu.make_async_copy(cot_part.at[own_half], cot.at[:, own_cols], half_sem.at[1])
+    cot_sent = to_mate(cot_part.at[mate_half], cot.at[:, own_cols], 1)
+
+    def attn_swap(i):
+        return to_mate(total.at[mate_block(i)], arrive_a.at[near(i)], 2 + i)
+
+    def normed_swap(i):
+        return to_mate(low.at[own_block(i)], low.at[own_block(i)], 2 + own_count + i)
+
+    def dense_swap(i):
+        return to_mate(total.at[mate_block(i)], arrive_b.at[near(i)], 2 + 2 * own_count + i)
+
+    def grad_swap(i):
+        return to_mate(low.at[own_block(i)], low.at[own_block(i)], 2 + 3 * own_count + i)
+
+    def hidden_swap(i):
+        return to_mate(total.at[mate_block(i)], arrive_a.at[near(i)], 2 + 4 * own_count + i)
+
+    def attn_grad_swap(i):
+        return to_mate(low.at[own_block(i)], low.at[own_block(i)], 2 + 5 * own_count + i)
+
+    def layer_swap(i):
+        return to_mate(stage.at[1, near(i)], layer_out.at[own_block(i)], 2 + 6 * own_count + i)
+
+    def token_swap(b):
+        return to_mate(total.at[near(b), pl.ds(0, part)], token_recv.at[near(b)], 2 + 7 * own_count + b)
+
+    small_swap = 2 + 7 * own_count + blocks
+
+    def layer_put(i):
+        return pltpu.make_async_copy(stage.at[0, near(i)], layer_out.at[own_block(i)], out_sem.at[i])
+
     gather.start(0)
-    for i in range(2):
-        halves[i].start()
-        crossed[i].start()
-    for c in range(1, len(chunks)):
+    for copy in (token_own, token_sent, cot_own, cot_sent):
+        copy.start()
+    for c in range(1, count):
         gather.start(c)
-    outs = []
-
-    def put(source, target):
-        copy = pltpu.make_async_copy(source, target, out_sem.at[len(outs)])
-        copy.start()
-        outs.append(copy)
-
     sums[...] = jnp.zeros_like(sums)
-    halves[0].wait()
-    crossed[0].wait_recv()
+    unit_sums[...] = jnp.zeros_like(unit_sums)
+    head_sums[...] = jnp.zeros_like(head_sums)
+    token_own.wait()
+    token_sent.wait_recv()
 
     @pl.loop(0, blocks)
     def _(b):
         at = rows_at(b, rows)
         token_t[:, at] = token[at, :].T
 
-    put(token, token_out)
-    put(token_t, token_t_out)
+    value_t, ctx_t = pair_low, pair_wide
     lane_head = lax.broadcasted_iota(jnp.int32, (1, pair), 1) // size
     for p in range(pairs):
         gather.need(p)
@@ -701,10 +758,11 @@
             qkv[p, at, :] = made.astype(low_type)
             value_t[:, at] = made[:, 2 * pair :].T.astype(low_type)
 
-        gather.advance(1)
+        pace = gather_pace[min(p, len(gather_pace) - 2)]
+        gather.advance(pace[0])
 
         @pl.loop(0, 2)
-        def _(h, p=p):
+        def _(h, p=p, pace=pace):
             own = jnp.where(lane_head == h, size ** (-0.5), 0.0).astype(low_type)
             head_rows = rows_at(h, size)
             for b in range(blocks):
@@ -729,197 +787,126 @@
                     )
                 ctx_t[head_rows, b * rows : (b + 1) * rows] = found
                 lse[2 * p + h, :, b * rows : (b + 1) * rows] = peak + jnp.log(row_total)
-                if b % 2:
-                    for now in range(2):
+                for now in range(2):
+                    if b % 2 and pace[1 + 2 * now + b // 2]:
 
                         @pl.when(h == now)
                         def _():
-                            gather.advance(1)
+                            gather.advance(pace[1 + 2 * now + b // 2])
 
         @pl.loop(0, blocks)
         def _(b, p=p):
             at = rows_at(b, rows)
             ctx[at, p * pair : (p + 1) * pair] = ctx_t[:, at].T.astype(low_type)
 
-    put(qkv, qkv_out)
-    put(lse, lse_out)
-    put(ctx, ctx_out)
     gather.need(pairs)
-    put(wa, wa_out)
-    gate_columns = gate_row(head_gate, heads, size).astype(low_type)
-
-    def swap(source, target, start, b):
-        at = pl.ds(b * rows, rows) if isinstance(b, int) else rows_at(b, rows)
-        return send(source.at[at], target.at[at], (col_s, col_r), start + b, mate)
+    gate_columns = gate_row(head_gate, heads, size)
+    gate_low = gate_columns.astype(low_type)
 
     @pl.loop(0, blocks)
-    def _(b):
-        at = rows_at(b, rows)
-        attn_out[at, :] = dot_nt(ctx[at, :] * gate_columns, wa[pairs])
-        swap(attn_out, precv, 2, b).start()
-
-    gather.advance(1)
-    for b in range(blocks):
-        swap(attn_out, precv, 2, b).wait()
-
-        @pl.loop(b * rows // fine, (b + 1) * rows // fine)
-        def _(i):
-            at = rows_at(i, fine)
-            attn = attn_out[at, :] + precv[at, :] + out_bias
-            attn_out[at, :] = attn
-            first, _ = norm_parts(token[at, :].astype(wide) + attn_gate * hidden * attn)
-            out = first * first_gain + first_shift
-            normed[at, :] = out
-            normed_low[at, :] = out.astype(low_type)
-
-    put(attn_out, attn_out_out)
-    gather.advance(1)
+    def _(t):
+        at = rows_at(mate_first(t), rows)
+        total[at, :] = dot_nt(ctx[at, :] * gate_low, wa[pairs])
+
+        @pl.when(t < own_count)
+        def _():
+            attn_swap(t).start()
+
+    gather.advance(gather_pace[-1][0])
+    gate_cols = attn_gate * hidden
+    for i in range(own_count):
+        attn_swap(i).wait_recv()
+
+        @pl.loop(i * rows // fine, (i + 1) * rows // fine)
+        def _(k):
+            here = rows_at(k, fine)
+            at = pl.ds(pl.multiple_of(place.col * (length // 2) + k * fine, fine), fine)
+            attn = total[at, :] + arrive_a[here, :] + out_bias
+            attn_out[here, :] = attn
+            normed, _ = norm_parts(token[at, :].astype(wide) + gate_cols * attn)
+            out = normed * first_gain + first_shift
+            second[here, :] = out
+            low[at, :] = out.astype(low_type)
+
+        normed_swap(i).start()
+    gather.advance(gather_pace[-1][1])
+
+    masks = [unit_row[:, j * group : (j + 1) * group] for j in range(2)]
     for j in range(2):
         gather.need(pairs + 1 + 2 * j)
         bias_row = up_bias[:, j * group : (j + 1) * group]
-        unit_mask = unit_row[:, j * group : (j + 1) * group].astype(low_type)
 
         @pl.loop(0, blocks)
-        def _(b, j=j, bias_row=bias_row):
-            at = rows_at(b, rows)
-            pre = dot_nn(normed_low[at, :], wm[2 * j]) + bias_row
+        def _(t, j=j, bias_row=bias_row):
+            at = rows_at(lax.rem(place.col * own_count + t, blocks), rows)
+            if j == 0:
+
+                @pl.when(t == own_count)
+                def _():
+                    for i in range(own_count):
+                        normed_swap(i).wait_recv()
+
+            pre = dot_nn(low[at, :], wm[2 * j]) + bias_row
             share = 0.5 * (1.0 + lax.erf(pre * (2.0 ** -0.5)))
             gelu[j, at, :] = (pre * share).astype(low_type)
             density = jnp.exp(-0.5 * pre * pre) * ((2.0 * math.pi) ** -0.5)
             slope[j, at, :] = (share + pre * density).astype(low_type)
             if j == 0:
-                normed_t[:, at] = normed_low[at, :].T
-
+                normed_t[:, at] = low[at, :].T
+
+        if j == 0:
+            for i in range(own_count):
+                attn_swap(i).wait_send()
+                normed_swap(i).wait_send()
         gather.need(pairs + 2 + 2 * j)
 
         @pl.loop(0, blocks)
-        def _(b, j=j, unit_mask=unit_mask):
-            at = rows_at(b, rows)
-            made = dot_nt(gelu[j, at, :] * unit_mask, wm[2 * j + 1])
+        def _(t, j=j):
+            at = rows_at(mate_first(t), rows)
+            made = dot_nt(gelu[j, at, :] * masks[j].astype(low_type), wm[2 * j + 1])
             if j == 0:
                 total[at, :] = made
             else:
                 total[at, :] += made
-                swap(total, drecv, 2 + blocks, b).start()
-
-    put(normed_t, normed_t_out)
-    put(gelu, gelu_out)
-    put(slope, slope_out)
-    put(wm, wm_out)
-    halves[1].wait()
-    crossed[1].wait_recv()
-    for b in range(blocks):
-        swap(total, drecv, 2 + blocks, b).wait_recv()
-
-        @pl.loop(b * rows // fine, (b + 1) * rows // fine)
-        def _(i):
-            at = rows_at(i, fine)
-            dense = total[at, :] + drecv[at, :] + down_bias
-            last, inverse = norm_parts(normed[at, :] + dense_gate * hidden * dense)
-            full = last * second_gain + second_shift
-            layer[at, :] = jnp.where(place.col == 0, full[:, :part], full[:, part:])
-            grad = cot[at, :].astype(wide)
+
+                @pl.when(t < own_count)
+                def _():
+                    dense_swap(t).start()
+
+    cot_own.wait()
+    cot_sent.wait_recv()
+    for i in range(own_count):
+        dense_swap(i).wait_recv()
+
+        @pl.loop(i * rows // fine, (i + 1) * rows // fine)
+        def _(k):
+            here = rows_at(k, fine)
+            at = pl.ds(pl.multiple_of(place.col * (length // 2) + k * fine, fine), fine)
+            dense = total[at, :] + arrive_b[here, :] + down_bias
+            normed, inverse = norm_parts(second[here, :] + dense_gate * hidden * dense)
+            full = normed * second_gain + second_shift
+            stage[0, here, :] = jnp.where(place.col == 0, full[:, :part], full[:, part:])
+            stage[1, here, :] = jnp.where(place.col == 0, full[:, part:], full[:, :part])
+            grad = cot[here, :].astype(wide)
             scaled = grad * second_gain
             one = jnp.mean(scaled, axis=1, keepdims=True)
-            two = jnp.mean(scaled * last, axis=1, keepdims=True)
-            made = inverse * (scaled - one - last * two)
-            second[at, :] = made
+            two = jnp.mean(scaled * normed, axis=1, keepdims=True)
+            made = inverse * (scaled - one - normed * two)
+            second[here, :] = made
             gated = (dense_gate * hidden * made).astype(low_type)
-            dense_low[at, :] = gated
-            product = dense * made
-            sums[0] += fold_rows(grad * last)
+            low[at, :] = gated
+            sums[0] += fold_rows(grad * normed)
             sums[1] += fold_rows(grad)
             sums[2] += fold_rows(gated.astype(wide))
-            sums[3] += fold_rows(product)
-
-        at = pl.ds(b * rows, rows)
-        dense_t[:, at] = dense_low[at, :].T
-
-    put(layer, layer_out)
-    put(second, second_out)
-    put(dense_low, dense_out_low)
-    put(dense_t, dense_t_out)
-    put(sums, sums_out)
-    gather.finish()
-    for copy in crossed:
-        copy.wait_send()
-    for b in range(blocks):
-        swap(total, drecv, 2 + blocks, b).wait_send()
-    for copy in outs:
-        copy.wait()
-
-
-def backward_kernel(
-    cut,
-    wa_in, wm_in, token_in, token_t_in, qkv_in, lse_in, ctx_in, attn_out_in, normed_t_in,
-    gelu_in, slope_in, second_in, dense_low_in, dense_t_in, sums_in,
-    first_gain, hidden_gate, unit_gate, head_gate, attention_gate, feedforward_gate, prefix_length,
-    grad_token, small_out, *rest,
-):
-    length, width, heads, size = cut.length, cut.width, cut.heads, cut.size
-    part, rows, fine = cut.part_width, cut.rows, cut.fine
-    blocks = length // rows
-    pair = 2 * size
-    pairs = heads // 2
-    count = pairs + 5
-    rest = list(rest)
-
-    def take(number):
-        taken = rest[:number]
-        del rest[:number]
-        return taken
-
-    grads = take(count)
-    (wa, wm, token, token_t, qkv, lse, ctx, attn_out, normed_t, gelu, slope, second, dense_low, dense_t, sums) = take(15)
-    (total, precv, fsend, frecv, ctx_grad, triple, key_grad, value_grad, query_t, key_t) = take(10)
-    (small, small_x, small_y, small_z, unit_sums, head_sums) = take(6)
-    buffers, first, mid_send, mid, last_send, last = (take(count) for _ in range(6))
-    (in_sem, one_s, one_r, two_s, two_r, z_s, z_r, col_s, col_r, small_s, small_r) = take(11)
-    place = Place(cut.row_size)
-    loads = {}
-    for i, (name, source, target) in enumerate(
-        (
-            ("dense_t", dense_t_in, dense_t),
-            ("gelu", gelu_in, gelu),
-            ("dense_low", dense_low_in, dense_low),
-            ("wm", wm_in, wm),
-            ("slope", slope_in, slope),
-            ("normed_t", normed_t_in, normed_t),
-            ("sums", sums_in, sums),
-            ("second", second_in, second),
-            ("attn_out", attn_out_in, attn_out),
-            ("token", token_in, token),
-            ("wa", wa_in, wa),
-            ("ctx", ctx_in, ctx),
-            ("qkv", qkv_in, qkv),
-            ("lse", lse_in, lse),
-            ("token_t", token_t_in, token_t),
-        )
-    ):
-        loads[name] = pltpu.make_async_copy(source, target, in_sem.at[i])
-        loads[name].start()
-
-    def load(*names):
-        for name in names:
-            loads[name].wait()
-
-    place.barrier()
-    prefix = prefix_length[0]
-    attn_gate, dense_gate = attention_gate[0].astype(wide), feedforward_gate[0].astype(wide)
-    hidden, unit_row = flat_row(hidden_gate).astype(wide), flat_row(unit_gate).astype(wide)
-    first_gain = flat_row(first_gain)
-    mate = place.col_mate()
-    scatter = Scatter(
-        place, buffers, grads, scatter_order(pairs), first, mid_send, mid, last_send, last,
-        (one_s, one_r), (two_s, two_r), (z_s, z_r),
-    )
-    unit_sums[...] = jnp.zeros_like(unit_sums)
-    head_sums[...] = jnp.zeros_like(head_sums)
-    group = wm.shape[2]
-
-    def swap(source, target, start, b):
-        at = pl.ds(b * rows, rows) if isinstance(b, int) else rows_at(b, rows)
-        return send(source.at[at], target.at[at], (col_s, col_r), start + b, mate)
+            sums[3] += fold_rows(dense * made)
+
+        grad_swap(i).start()
+        dense_t[:, own_block(i)] = low[own_block(i), :].T
+    for i in range(own_count):
+        layer_swap(i).start()
+        layer_put(i).start()
+        grad_swap(i).wait_recv()
+        dense_t[:, mate_block(i)] = low[mate_block(i), :].T
 
     def product(target, left, right, mask=None):
         @pl.loop(0, width // rows)
@@ -928,18 +915,17 @@
             made = dot_nn(left[at, :], right[...])
             target[at, :] = (made if mask is None else made * mask).astype(low_type)
 
-    masks = [unit_row[:, j * group : (j + 1) * group] for j in range(2)]
-    load("dense_t", "gelu")
     for j in range(2):
         product(buffers[j], dense_t, gelu.at[j], masks[j])
         scatter.begin(j)
-    load("dense_low", "wm", "slope")
+    for i in range(own_count):
+        dense_swap(i).wait_send()
     for j in range(2):
 
         @pl.loop(0, blocks)
-        def _(b, j=j):
-            at = rows_at(b, rows)
-            inner = dot_nn(dense_low[at, :], wm[2 * j + 1]).astype(low_type).astype(wide)
+        def _(t, j=j):
+            at = rows_at(mate_first(t), rows)
+            inner = dot_nn(low[at, :], wm[2 * j + 1]).astype(low_type).astype(wide)
             unit_sums[2 + j] += fold_rows(gelu[j, at, :].astype(wide) * inner)
             pre = (masks[j] * inner * slope[j, at, :].astype(wide)).astype(low_type)
             slope[j, at, :] = pre
@@ -949,51 +935,50 @@
                 total[at, :] = made
             else:
                 total[at, :] += made
-                swap(total, precv, 0, b).start()
-
-        scatter.advance(1)
-        if j == 0:
-            load("normed_t")
+
+                @pl.when(t < own_count)
+                def _():
+                    hidden_swap(t).start()
+
+        scatter.advance(scatter_pace[0][j])
         product(buffers[2 + j], normed_t, slope.at[j])
         scatter.begin(2 + j)
 
-    load("sums", "second", "attn_out", "token")
-    for b in range(blocks):
-        swap(total, precv, 0, b).wait_recv()
-
-        @pl.loop(b * rows // fine, (b + 1) * rows // fine)
-        def _(i):
-            at = rows_at(i, fine)
-            attn = attn_out[at, :]
-            gate_cols = attn_gate * hidden
+    for i in range(own_count):
+        grad_swap(i).wait_send()
+    for i in range(own_count):
+        hidden_swap(i).wait_recv()
+
+        @pl.loop(i * rows // fine, (i + 1) * rows // fine)
+        def _(k):
+            here = rows_at(k, fine)
+            at = pl.ds(pl.multiple_of(place.col * (length // 2) + k * fine, fine), fine)
+            attn = attn_out[here, :]
             normed, inverse = norm_parts(token[at, :].astype(wide) + gate_cols * attn)
-            grad = second[at, :] + (total[at, :] + precv[at, :])
+            grad = second[here, :] + (total[at, :] + arrive_a[here, :])
             scaled = grad * first_gain
             one = jnp.mean(scaled, axis=1, keepdims=True)
             two = jnp.mean(scaled * normed, axis=1, keepdims=True)
             made = inverse * (scaled - one - normed * two)
-            second[at, :] = made
+            second[here, :] = made
             gated = (gate_cols * made).astype(low_type)
-            dense_low[at, :] = gated
+            low[at, :] = gated
             sums[4] += fold_rows(grad * normed)
             sums[5] += fold_rows(grad)
             sums[6] += fold_rows(gated.astype(wide))
             sums[7] += fold_rows(attn * made)
 
-        at = pl.ds(b * rows, rows)
-        dense_t[:, at] = dense_low[at, :].T
-        if b % 2:
-            scatter.advance(1)
-
-    for b in range(blocks):
-        swap(total, precv, 0, b).wait_send()
-    load("wa", "ctx", "qkv", "lse", "token_t")
-    gate_columns = gate_row(head_gate, heads, size)
+        attn_grad_swap(i).start()
+        dense_t[:, own_block(i)] = low[own_block(i), :].T
+        scatter.advance(scatter_pace[1][i])
+    for i in range(own_count):
+        attn_grad_swap(i).wait_recv()
+        dense_t[:, mate_block(i)] = low[mate_block(i), :].T
 
     @pl.loop(0, blocks)
     def _(b):
         at = rows_at(b, rows)
-        gated = dot_nn(dense_low[at, :], wa[pairs]).astype(low_type).astype(wide)
+        gated = dot_nn(low[at, :], wa[pairs]).astype(low_type).astype(wide)
         seen = ctx[at, :].astype(wide)
         head_sums[...] += fold_rows(seen * gated)
         ctx_grad[at, :] = (gated * gate_columns).astype(low_type)
@@ -1001,8 +986,12 @@
 
     product(buffers[4], dense_t, ctx)
     scatter.begin(4)
-    scatter.advance(1)
-    lane_head = lax.broadcasted_iota(jnp.int32, (1, pair), 1) // size
+    scatter.advance(scatter_pace[2][0])
+    for i in range(own_count):
+        hidden_swap(i).wait_send()
+        layer_put(i).wait()
+        layer_swap(i).wait()
+    key_t, query_t = pair_low, pair_wide
     bias_sums = []
     for p in range(pairs):
 
@@ -1013,9 +1002,10 @@
 
         key_grad[...] = jnp.zeros_like(key_grad)
         value_grad[...] = jnp.zeros_like(value_grad)
+        pace = scatter_pace[3 + min(p, len(scatter_pace) - 4)]
 
         @pl.loop(0, 2)
-        def _(h, p=p):
+        def _(h, p=p, pace=pace):
             own = jnp.where(lane_head == h, size ** (-0.5), 0.0).astype(low_type)
             one_head = jnp.where(lane_head == h, 1.0, 0.0).astype(low_type)
             head_rows = rows_at(h, size)
@@ -1040,12 +1030,12 @@
                     key_grad[at, :] += dot_nn(grad_score, query)
                     found = found + dot_nn(key_t[head_rows, at], grad_score)
                 query_t[head_rows, b * rows : (b + 1) * rows] = found * size ** (-0.5)
-                if b % 2:
-                    for now in range(2):
+                for now in range(2):
+                    if b % 2 and pace[2 * now + b // 2]:
 
                         @pl.when(h == now)
                         def _():
-                            scatter.advance(1)
+                            scatter.advance(pace[2 * now + b // 2])
 
         query_sum = jnp.zeros((8, pair), wide)
         value_sum = jnp.zeros((8, pair), wide)
@@ -1061,11 +1051,11 @@
         bias_sums.append((query_sum, value_sum))
         product(buffers[5 + p], token_t, triple)
         scatter.begin(5 + p)
-        if p < pairs - 1:
-            scatter.advance(1)
+        scatter.advance(pace[4])
 
         @pl.loop(0, blocks)
-        def _(b, p=p):
+        def _(t, p=p):
+            b = mate_first(t)
             at = rows_at(b, rows)
             made = dot_nt(triple[at, :], wa[p])
             if p > 0:
@@ -1073,12 +1063,11 @@
             if p < pairs - 1:
                 total[at, :] = made
             else:
-                mine = jnp.where(place.col == 0, made[:, :part], made[:, part:])
-                other = jnp.where(place.col == 0, made[:, part:], made[:, :part])
-                kept = second[at, :]
-                grad_token[at, :] = mine + jnp.where(place.col == 0, kept[:, :part], kept[:, part:])
-                fsend[at, :] = other.astype(low_type)
-                swap(fsend, frecv, blocks, b).start()
+                kept = second[rows_at(lax.rem(t, own_count), rows), :]
+                made = made + jnp.where(t >= own_count, kept, 0.0)
+                total[at, :part] = jnp.where(place.col == 0, made[:, part:], made[:, :part])
+                total[at, part:] = jnp.where(place.col == 0, made[:, :part], made[:, part:])
+                token_swap(b).start()
 
     def whole(values):
         return jnp.sum(values, axis=0, keepdims=True)
@@ -1105,11 +1094,16 @@
     small[13:14, :part] = whole(head_sums[...])
     small[13:14, part:] = jnp.zeros((1, part), wide)
     small[14:16, :] = jnp.zeros((2, width), wide)
-    copy_x = send(small, small_x.at[0], (small_s, small_r), 0, place.x_mate())
+    copy_c = to_mate(small.at[pl.ds(0, 8)], small_c.at[0, pl.ds(0, 8)], small_swap)
+    copy_c.start()
+    copy_c.wait_recv()
+    small_c[1, 0:8, :] = small[0:8, :] + small_c[0, 0:8, :]
+    small_c[1, 8:16, :] = small[8:16, :]
+    copy_x = send(small_c.at[1], small_x.at[0], (small_s, small_r), 0, place.x_mate())
     copy_x.start()
     scatter.advance(1)
     copy_x.wait_recv()
-    small_x[1] = small[...] + small_x[0]
+    small_x[1] = small_c[1] + small_x[0]
     copy_y = send(small_x.at[1], small_y.at[0], (small_s, small_r), 1, place.y_mate())
     copy_y.start()
     scatter.advance(1)
@@ -1124,9 +1118,12 @@
     for copy in copies:
         copy.start()
     for b in range(blocks):
-        swap(fsend, frecv, blocks, b).wait_recv()
-        at = pl.ds(b * rows, rows)
-        grad_token[at, :] += frecv[at, :].astype(wide)
+        token_swap(b).wait_recv()
+        found = total[near(b), part:] + token_recv[near(b), :]
+        stage[b // own_count, near(b % own_count), :] = found
+        pltpu.make_async_copy(
+            stage.at[b // own_count, near(b % own_count)], token_out.at[near(b)], out_sem.at[own_count + b]
+        ).start()
     scatter.finish()
     for copy in copies:
         copy.wait_recv()
@@ -1134,10 +1131,16 @@
     for z in range(1, cut.row_size):
         result = result + small_z[z]
     small_out[...] = result
-    for copy in [copy_x, copy_y] + copies:
+    gather.finish()
+    for copy in [token_sent, cot_sent, copy_c, copy_x, copy_y] + copies:
         copy.wait_send()
+    for i in range(own_count):
+        attn_grad_swap(i).wait_send()
     for b in range(blocks):
-        swap(fsend, frecv, blocks, b).wait_send()
+        token_swap(b).wait_send()
+        pltpu.make_async_copy(
+            stage.at[b // own_count, near(b % own_count)], token_out.at[near(b)], out_sem.at[own_count + b]
+        ).wait()
 
 
 def place_kernel(
@@ -1185,12 +1188,11 @@
 
 
 def scatter_order(pairs):
-    out = [(0, 0), (0, 1), (0, 2), (1, 0), (1, 1), (0, 3), (2, 0), (1, 2), (2, 1), (1, 3), (0, 4), (2, 2), (1, 4), (2, 3)]
-    before = 4
-    for c in range(5, 5 + pairs):
-        out += [(0, c), (2, before), (1, c)]
-        before = c
-    return out + [(2, before)]
+    return [(0, 0), (0, 1), (1, 0), (0, 2), (1, 1), (2, 0), (0, 3), (0, 4), (1, 2), (2, 1), (0, 5), (1, 3), (1, 5), (0, 6), (1, 4), (0, 7), (2, 2), (1, 6), (2, 3), (1, 7), (2, 5), (2, 4), (2, 6), (2, 7)]
+
+
+gather_pace = ((1, 1, 0, 1, 0), (1, 1, 1, 1, 1), (1, 0, 1, 0, 1), (1, 1))
+scatter_pace = ((1, 1), (0, 0), (0,), (1, 0, 0, 1, 0), (2, 1, 1, 1, 0), (1, 2, 0, 0, 1))
 
 
 class Cut(NamedTuple):
@@ -1234,76 +1236,47 @@
 vmem_most = 67043328
 
 
-def run_forward(cut, token_part, cot_part, *args):
-    length, width, half = cut.length, cut.width, cut.part_width
-    group = cut.units // 2
-    chunks_a, chunks = cut.heads // 2 + 1, cut.heads // 2 + 5
-    blocks = length // cut.rows
-    kept = [
-        ((chunks_a, width, half), low_type),
-        ((4, width, group), low_type),
-        ((length, width), low_type),
-        ((width, length), low_type),
-        ((cut.heads // 2, length, half), low_type),
-        ((cut.heads, 1, length), wide),
-        ((length, half), low_type),
-        ((length, width), wide),
-        ((width, length), low_type),
-        ((2, length, group), low_type),
-        ((2, length, group), low_type),
-        ((length, half), wide),
-        ((length, width), wide),
-        ((length, width), low_type),
-        ((width, length), low_type),
-        ((8, 8, width), wide),
-    ]
-    own = [
-        ((length, width), low_type),
-        ((2 * cut.size, length), low_type),
-        ((2 * cut.size, length), wide),
-        ((length, width), wide),
-        ((length, width), low_type),
-        ((length, width), wide),
-        ((length, width), wide),
-        ((length, width), wide),
-        ((chunks_a, cut.part, half), low_type),
-        ((4, cut.part, group), low_type),
-    ]
-    z = cut.row_size - 1
-    semaphores = [dma(chunks), dma(chunks, z), dma(chunks, z), dma(chunks, 2), dma(chunks, 2), dma(chunks, 4), dma(chunks, 4)]
-    semaphores += [dma(2 + 2 * blocks), dma(2 + 2 * blocks), dma(2), dma(len(kept))]
-    return pl.pallas_call(
-        partial(forward_kernel, cut),
-        out_shape=like(kept),
-        in_specs=[any_spec()] * 2 + [vmem_spec()] * (len(args) - 4) + [smem_spec()] * 4,
-        out_specs=[any_spec()] * len(kept),
-        scratch_shapes=scratch(kept) + scratch(own) + semaphores,
-        compiler_params=pltpu.CompilerParams(collective_id=0, has_side_effects=True, vmem_limit_bytes=vmem_most),
-        name="layer_forward",
-    )(token_part, cot_part, *args)
-
-
-def run_backward(cut, kept, *args):
+def run_layer(cut, *args):
     length, width, half = cut.length, cut.width, cut.part_width
     group = cut.units // 2
     pairs = cut.heads // 2
     blocks = length // cut.rows
     columns = [group] * 4 + [half] * (pairs + 1)
     count = len(columns)
-    outs = [((length, half), wide), ((16, width), wide)] + [((cut.part, n), wide) for n in columns]
-    loaded = [(item.shape, item.dtype) for item in kept]
+    outs = [((length, half), wide), ((length, half), wide), ((16, width), wide)]
+    outs += [((cut.part, n), wide) for n in columns]
     own = [
+        ((pairs + 1, width, half), low_type),
+        ((4, width, group), low_type),
+        ((length, width), low_type),
+        ((width, length), low_type),
+        ((pairs, length, half), low_type),
+        ((cut.heads, 1, length), wide),
+        ((length, half), low_type),
+        ((length // 2, width), wide),
+        ((width, length), low_type),
+        ((2, length, group), low_type),
+        ((2, length, group), low_type),
+        ((length // 2, width), wide),
+        ((length, width), low_type),
+        ((width, length), low_type),
+        ((8, 8, width), wide),
+        ((length // 2, width), low_type),
         ((length, width), wide),
-        ((length, width), wide),
-        ((length, half), low_type),
-        ((length, half), low_type),
+        ((length // 2, width), wide),
+        ((length // 2, width), wide),
+        ((2, length // 2, half), wide),
+        ((length, half), wide),
         ((length, half), low_type),
         ((length, half), low_type),
         ((length, 2 * cut.size), wide),
         ((length, 2 * cut.size), wide),
         ((2 * cut.size, length), wide),
         ((2 * cut.size, length), low_type),
+        ((pairs + 1, cut.part, half), low_type),
+        ((4, cut.part, group), low_type),
         ((16, width), wide),
+        ((2, 16, width), wide),
         ((2, 16, width), wide),
         ((2, 16, width), wide),
         ((cut.row_size, 16, width), wide),
@@ -1318,17 +1291,20 @@
     own += [((2 * quarter, n), low_type) for n in columns]
     own += [((cut.row_size - 1, cut.part, n), low_type) for n in columns]
     z = cut.row_size - 1
-    semaphores = [dma(len(kept)), dma(count, 4), dma(count, 4), dma(count, 2), dma(count, 2), dma(count, z), dma(count, z)]
-    semaphores += [dma(2 * blocks), dma(2 * blocks), dma(2 + z), dma(2 + z)]
+    semaphores = [dma(count), dma(count, z), dma(count, z), dma(count, 2), dma(count, 2), dma(count, 4), dma(count, 4)]
+    semaphores += [dma(2), dma(blocks // 2 + blocks)]
+    semaphores += [dma(count, 4), dma(count, 4), dma(count, 2), dma(count, 2), dma(count, z), dma(count, z)]
+    pair_swaps = 3 + 7 * (blocks // 2) + blocks
+    semaphores += [dma(pair_swaps), dma(pair_swaps), dma(2 + z), dma(2 + z)]
     return pl.pallas_call(
-        partial(backward_kernel, cut),
+        partial(layer_kernel, cut),
         out_shape=like(outs),
-        in_specs=[any_spec()] * len(kept) + [vmem_spec()] * 3 + [smem_spec()] * 4,
-        out_specs=[vmem_spec()] * len(outs),
-        scratch_shapes=scratch(loaded) + scratch(own) + semaphores,
-        compiler_params=pltpu.CompilerParams(collective_id=1, has_side_effects=True, vmem_limit_bytes=vmem_most),
-        name="layer_backward",
-    )(*kept, *args)
+        in_specs=[any_spec()] * 2 + [vmem_spec()] * (len(args) - 6) + [smem_spec()] * 4,
+        out_specs=[any_spec()] * 2 + [vmem_spec()] * (len(outs) - 2),
+        scratch_shapes=scratch(own) + semaphores,
+        compiler_params=pltpu.CompilerParams(collective_id=0, has_side_effects=True, vmem_limit_bytes=vmem_most),
+        name="whole_layer",
+    )(*args)
 
 
 def fused_device(
@@ -1344,20 +1320,17 @@
     ]
     scalars = [head_gate, attention_gate, feedforward_gate, prefix_length]
     weights = [qkv_weight, out_weight.T, up_weight, down_weight.T]
-    kept = list(run_forward(cut, tokens, cotangent, *weights, *rows, *scalars))
-    layer_out = kept.pop(11)
-    made = run_backward(cut, kept, rows[5], rows[9], rows[10], *scalars)
-    grad_tokens, small = made[0], made[1]
+    layer_out, grad_tokens, *made = run_layer(cut, tokens, cotangent, *weights, *rows, *scalars)
     seq_total = lax.axis_size(("dp", "row"))
     lanes = [half, half, width, units, width, width, width, width, width, cut.heads, width, units, seq_total, seq_total]
     shapes = [(3, part, half), (part, half), (part, units), (part, units)] + [(n,) for n in lanes]
     outs = pl.pallas_call(
         partial(place_kernel, cut),
         out_shape=like([(shape, wide) for shape in shapes]),
-        in_specs=[vmem_spec()] * (len(made) - 1),
+        in_specs=[vmem_spec()] * len(made),
         out_specs=[vmem_spec()] * len(shapes),
         name="place_results",
-    )(small, *made[2:])
+    )(*made)
     return (layer_out, grad_tokens, outs[0], outs[1].T, outs[2], outs[3].T, *outs[4:])
 
 

time: 197 us -> 171 us (0.87)
  Pallas kernels: 190 us -> 164 us
    pallas_call x2 -> x1, Pallas kernels: 188 us -> 162 us  [run_layer(): pl.pallas_call(partial(layer_kernel, cut), out_shape=like(outs), in_specs...]
where the time goes in v1:
time: 171 us
  Pallas kernels  164 us (96%)
  local copies, waits for them, and re-layouts  3.92 us (2%)
  between operations  2.63 us (2%)
    pallas_call x1, Pallas kernels, run_layer(): pl.pallas_call(partial(layer_kernel, cut), out_shape=like(outs), in_specs...  162 us
    unnamed x4, local copies, waits for them, and re-layouts  3.92 us

profile of v1, /device:TPU:0, one launch (start us, length us, event | category | flops | bytes accessed | tf_op | source)
XLA Modules:
  0.0 170.8 jit_solution(4804306479863639781)
XLA Ops:
  2.6 162.1 %whole_layer.1 = (f32[1024,384]{1,0:T(8,128)}, f32[1024,384]{1,0:T(8,128)}, f32[16,768]{1,0:T(8,128)}, f32[48,768]{1,0:T(8,128)}, f32[48,768]{1,0:T(8,128)}, /*i...) custom-call(bf16[1024,384]{1,0:T(8,128)(2,1)} %token_part.1, ...), custom_call_target="tpu_custom_call" | custom-call | tf_op jit(solution)/shard_map/whole_layer/pallas_call | solution.py:1299
  164.7 2.2 %place_results.1 = (f32[3,48,384]{2,1,0:T(8,128)}, f32[48,384]{1,0:T(8,128)}, f32[48,1536]{1,0:T(8,128)}, f32[48,1536]{1,0:T(8,128)}, f32[384]{0:T(512)}, /*inde...) custom-call(f32[16,768]{1,0:T(8,128)} %get-tuple-element.51.small, ...), custom_call_target="tpu_custom_call" | custom-call | tf_op jit(solution)/shard_map/place_results/pallas_call | solution.py:1327
  166.9 0.0 copy-start
  166.9 2.8 %copy.46 = f32[1024,384]{1,0:T(8,128)} copy(f32[1024,384]{1,0:T(8,128)} %get-tuple-element.98) | data formatting | bytes 3145728
  169.7 0.0 copy-done
  169.7 1.1 copy.47
Async XLA Ops:
  166.9 2.8 %copy-start = (f32[1024,384]{1,0:T(8,128)S(1)}, f32[1024,384]{1,0:T(8,128)}, u32[]{:S(2)}) copy-start(f32[1024,384]{1,0:T(8,128)} %get-tuple-element.99) | copy-start | bytes 4718596

commit v2 on v1

--- a/solution.py
+++ b/solution.py
@@ -410,69 +410,100 @@
 
 
 class Gather:
-    def __init__(self, place, shards, chunks, order, own_sem, z_sems, two_sems, three_sems):
-        self.place, self.shards, self.chunks = place, shards, chunks
+    def __init__(self, place, shards, chunks, turned, order, own_sem, z_sems, two_sems, three_sems, turned_sems):
+        self.place, self.shards, self.chunks, self.turned = place, shards, chunks, turned
         self.own_sem, self.z_sems, self.two_sems, self.three_sems = own_sem, z_sems, two_sems, three_sems
+        self.turned_sems = turned_sems
         self.part = shards[0].shape[0]
         self.block = self.part * place.row_size
         self.half = self.block // 2
         self.steps, self.done = order, 0
 
+    def block_rows(self, dp):
+        return pl.ds(pl.multiple_of(dp * self.block, 16), self.block)
+
     def half_rows(self, dp, half):
         return pl.ds(pl.multiple_of(dp * self.block + half * self.half, 16), self.half)
 
-    def own_rows(self):
-        place = self.place
-        return pl.ds(pl.multiple_of(place.dp * self.block + place.row * self.part, 16), self.part)
+    def part_rows(self, dp):
+        return pl.ds(pl.multiple_of(dp * self.block + self.place.row * self.part, 16), self.part)
+
+    def half_cols(self, c, half):
+        count = self.chunks[c].shape[1] // 2
+        return pl.ds(half * count, count)
 
     def own(self, c):
-        return pltpu.make_async_copy(self.shards[c], self.chunks[c].at[self.own_rows()], self.own_sem.at[c])
+        rows = self.part_rows(self.place.dp)
+        return pltpu.make_async_copy(self.shards[c], self.chunks[c].at[rows], self.own_sem.at[c])
 
     def along_z(self, c):
-        place = self.place
+        place, rows = self.place, self.part_rows(self.place.dp)
         return [
-            send(
-                self.shards[c], self.chunks[c].at[self.own_rows()], self.z_sems, (c, step - 1), place.row_mate(step)
-            )
+            send(self.shards[c], self.chunks[c].at[rows], self.z_sems, (c, step - 1), place.row_mate(step))
             for step in range(1, place.row_size)
         ]
 
-    def pass_on(self, c, dp, half, sems, index, mate):
-        at = self.chunks[c].at[self.half_rows(dp, half)]
-        return send(at, at, sems, (c, index), mate)
+    def turned_z(self, c):
+        place, found = self.place, []
+        for step in range(1, place.row_size):
+            for half, dp in ((0, place.x_dp), (1, place.y_dp)):
+                at = self.chunks[c].at[self.part_rows(dp), self.half_cols(c, half)]
+                found.append(send(at, at, self.turned_sems, (c, 2 * step - 2 + half), place.row_mate(step)))
+        return found
 
     def second(self, c):
-        place = self.place
-        return [
-            self.pass_on(c, place.dp, 0, self.two_sems, 0, place.x_mate()),
-            self.pass_on(c, place.dp, 1, self.two_sems, 1, place.y_mate()),
-        ]
+        place, chunk, found = self.place, self.chunks[c], []
+        for half, mate in ((0, place.x_mate()), (1, place.y_mate())):
+            if c in self.turned:
+                cols = self.half_cols(c, half)
+                source, target = self.shards[c].at[:, cols], chunk.at[self.part_rows(place.dp), cols]
+            else:
+                source = target = chunk.at[self.half_rows(place.dp, half)]
+            found.append(send(source, target, self.two_sems, (c, half), mate))
+        return found
 
     def third(self, c):
-        place = self.place
-        return [
-            self.pass_on(c, place.dp, 0, self.three_sems, 0, place.y_mate()),
-            self.pass_on(c, place.dp, 1, self.three_sems, 2, place.x_mate()),
-            self.pass_on(c, place.x_dp, 0, self.three_sems, 1, place.y_mate()),
-            self.pass_on(c, place.y_dp, 1, self.three_sems, 3, place.x_mate()),
-        ]
-
-    def start(self, c):
-        self.own(c).start()
-        for copy in self.along_z(c):
-            copy.start()
+        place, chunk, found = self.place, self.chunks[c], []
+        for index, (dp, half, mate) in enumerate(
+            (
+                (place.dp, 0, place.y_mate()),
+                (place.dp, 1, place.x_mate()),
+                (place.x_dp, 0, place.y_mate()),
+                (place.y_dp, 1, place.x_mate()),
+            )
+        ):
+            if c in self.turned:
+                at = chunk.at[self.block_rows(dp), self.half_cols(c, half)]
+            else:
+                at = chunk.at[self.half_rows(dp, half)]
+            found.append(send(at, at, self.three_sems, (c, index), mate))
+        return found
 
     def step(self):
         stage, c = self.steps[self.done]
         self.done += 1
-        if stage == 0:
+        if stage < 0:
+            self.own(c).start()
+            for copy in self.along_z(c) + (self.second(c) if c in self.turned else []):
+                copy.start()
+        elif stage == 0 and c in self.turned:
+            for copy in self.second(c):
+                copy.wait_recv()
+            for copy in self.turned_z(c):
+                copy.start()
+        elif stage == 0:
             self.own(c).wait()
             for copy in self.along_z(c):
                 copy.wait_recv()
             for copy in self.second(c):
                 copy.start()
         elif stage == 1:
-            for copy in self.second(c):
+            if c in self.turned:
+                self.own(c).wait()
+                waits = self.along_z(c) + self.turned_z(c)
+            else:
+                waits = self.second(c)
+            for copy in waits:
                 copy.wait_recv()
             for copy in self.third(c):
                 copy.start()
@@ -480,6 +511,10 @@
             for copy in self.third(c):
                 copy.wait_recv()
 
+    def begin(self):
+        while self.steps[self.done][0] < 0:
+            self.step()
+
     def advance(self, count):
         for _ in range(count):
             if self.done < len(self.steps):
@@ -494,11 +529,15 @@
         for c in range(len(self.chunks)):
             for copy in self.along_z(c) + self.second(c) + self.third(c):
                 copy.wait_send()
+            for copy in self.turned_z(c) if c in self.turned else []:
+                copy.wait_send()
 
 
 class Scatter:
-    def __init__(self, place, chunks, outs, order, first, mid_send, mid, last_send, last, one_sems, two_sems, z_sems):
-        self.place, self.chunks, self.outs = place, chunks, outs
+    def __init__(
+        self, place, chunks, outs, turned, order, first, mid_send, mid, last_send, last, one_sems, two_sems, z_sems
+    ):
+        self.place, self.chunks, self.outs, self.turned = place, chunks, outs, turned
         self.first, self.mid_send, self.mid, self.last_send, self.last = first, mid_send, mid, last_send, last
         self.one_sems, self.two_sems, self.z_sems = one_sems, two_sems, z_sems
         self.part = outs[0].shape[0]
@@ -507,38 +546,51 @@
         self.count = len(chunks)
         self.steps, self.done, self.begun = order, 0, []
 
+    def block_rows(self, dp):
+        return pl.ds(pl.multiple_of(dp * self.block, 16), self.block)
+
     def half_rows(self, dp, half):
         return pl.ds(pl.multiple_of(dp * self.block + half * self.half, 16), self.half)
+
+    def z_rows(self, z):
+        return pl.ds(pl.multiple_of(z * self.part, 16), self.part)
+
+    def half_cols(self, c, half):
+        count = self.chunks[c].shape[1] // 2
+        return pl.ds(half * count, count)
 
     def one(self, c):
         place, chunk, first = self.place, self.chunks[c], self.first[c]
         found = []
         for i in range(2):
-            rows = self.half_rows((1 - place.y) * 2 + i, 0)
-            found.append(send(chunk.at[rows], first.at[0, i], self.one_sems, (c, i), place.y_mate()))
-            rows = self.half_rows(i * 2 + (1 - place.x), 1)
-            found.append(send(chunk.at[rows], first.at[1, i], self.one_sems, (c, 2 + i), place.x_mate()))
+            for half, dp, mate in (
+                (0, (1 - place.y) * 2 + i, place.y_mate()),
+                (1, i * 2 + (1 - place.x), place.x_mate()),
+            ):
+                if c in self.turned:
+                    at = chunk.at[self.block_rows(dp), self.half_cols(c, half)]
+                else:
+                    at = chunk.at[self.half_rows(dp, half)]
+                found.append(send(at, first.at[half, i], self.one_sems, (c, 2 * half + i), mate))
         return found
 
     def two(self, c):
-        place, mid_send, mid = self.place, self.mid_send[c], self.mid[c]
+        place = self.place
+        source, target = (self.last_send[c], self.last[c]) if c in self.turned else (self.mid_send[c], self.mid[c])
         return [
-            send(mid_send.at[0], mid.at[0], self.two_sems, (c, 0), place.x_mate()),
-            send(mid_send.at[1], mid.at[1], self.two_sems, (c, 1), place.y_mate()),
+            send(source.at[0], target.at[0], self.two_sems, (c, 0), place.x_mate()),
+            send(source.at[1], target.at[1], self.two_sems, (c, 1), place.y_mate()),
         ]
 
     def along_z(self, c):
-        place = self.place
-        found = []
+        place, found = self.place, []
         for step in range(1, place.row_size):
-            mate = lax.rem(place.row + step, place.row_size)
-            rows = pl.ds(pl.multiple_of(mate * self.part, 16), self.part)
-            found.append(
-                send(
-                    self.last_send[c].at[rows], self.last[c].at[step - 1], self.z_sems, (c, step - 1),
-                    place.row_mate(step),
-                )
-            )
+            rows = self.z_rows(lax.rem(place.row + step, place.row_size))
+            if c in self.turned:
+                source, target = self.mid_send[c].at[:, rows], self.mid[c].at[step - 1]
+            else:
+                source, target = self.last_send[c].at[rows], self.last[c].at[step - 1]
+            found.append(send(source, target, self.z_sems, (c, step - 1), place.row_mate(step)))
         return found
 
     def begin(self, c):
@@ -549,6 +601,9 @@
     def step(self):
         stage, c = self.steps[self.done]
         self.done += 1
+        if c in self.turned:
+            self.turned_step(stage, c)
+            return
         place, chunk = self.place, self.chunks[c]
         first, mid_send, mid = self.first[c], self.mid_send[c], self.mid[c]
         last_send, last = self.last_send[c], self.last[c]
@@ -575,11 +630,44 @@
             for copy in self.along_z(c):
                 copy.start()
         else:
-            total = last_send[pl.ds(pl.multiple_of(place.row * self.part, 16), self.part), :].astype(wide)
+            total = last_send[self.z_rows(place.row), :].astype(wide)
             for step, copy in enumerate(self.along_z(c)):
                 copy.wait_recv()
                 total = total + last[step].astype(wide)
             self.outs[c][...] = total
+
+    def turned_step(self, stage, c):
+        place, chunk, out = self.place, self.chunks[c], self.outs[c]
+        first, mid_send, mid = self.first[c], self.mid_send[c], self.mid[c]
+        last_send, last = self.last_send[c], self.last[c]
+        if stage == 0:
+            for copy in self.one(c):
+                copy.wait_recv()
+            for half in range(2):
+                for i in range(2):
+                    dp = place.y * 2 + i if half == 0 else i * 2 + place.x
+                    mine = chunk[self.block_rows(dp), self.half_cols(c, half)].astype(wide)
+                    mid_send[2 * half + i] = (mine + first[half, i].astype(wide)).astype(low_type)
+            for copy in self.along_z(c):
+                copy.start()
+        elif stage == 1:
+            for copy in self.along_z(c):
+                copy.wait_recv()
+            for half, slot in ((0, place.x), (1, place.y)):
+                for index, keep in ((slot, True), (1 - slot, False)):
+                    total = mid_send[2 * half + index, self.z_rows(place.row), :].astype(wide)
+                    for step in range(place.row_size - 1):
+                        total = total + mid[step, 2 * half + index].astype(wide)
+                    if keep:
+                        out[:, self.half_cols(c, half)] = total
+                    else:
+                        last_send[half] = total.astype(low_type)
+            for copy in self.two(c):
+                copy.start()
+        else:
+            for half, copy in enumerate(self.two(c)):
+                copy.wait_recv()
+                out[:, self.half_cols(c, half)] += last[half].astype(wide)
 
     def advance(self, count):
         for _ in range(count):
@@ -639,11 +727,12 @@
 
     grads = take(count)
     (wa, wm, token, token_t, qkv, lse, ctx, attn_out, normed_t, gelu, slope, second, low, dense_t, sums) = take(15)
-    (cot, total, arrive_a, arrive_b, stage, token_recv, ctx_grad, triple, key_grad, value_grad) = take(10)
-    (pair_wide, pair_low, shards_a, shards_m) = take(4)
+    (cot, total, arrive_a, arrive_b, stage, token_recv, ctx_grad, key_grad, value_grad) = take(9)
+    (pair_wide, pair_low, key_t, shards_a, shards_m) = take(5)
     (small, small_c, small_x, small_y, small_z, unit_sums, head_sums) = take(7)
     buffers, first, mid_send, mid, last_send, last = (take(count) for _ in range(6))
-    (own_sem, gz_s, gz_r, g2_s, g2_r, g3_s, g3_r, half_sem, out_sem, s1_s, s1_r, s2_s, s2_r, sz_s, sz_r) = take(15)
+    (own_sem, gz_s, gz_r, g2_s, g2_r, g3_s, g3_r, gt_s, gt_r, half_sem, out_sem) = take(11)
+    (s1_s, s1_r, s2_s, s2_r, sz_s, sz_r) = take(6)
     (col_s, col_r, small_s, small_r) = take(4)
     group = wm.shape[2]
     place = Place(cut.row_size)
@@ -667,10 +756,11 @@
     chunks = [wa.at[i] for i in range(pairs + 1)] + [wm.at[i] for i in range(4)]
     shards = [shards_a.at[i] for i in range(pairs + 1)] + [shards_m.at[i] for i in range(4)]
     gather = Gather(
-        place, shards, chunks, gather_order(count), own_sem, (gz_s, gz_r), (g2_s, g2_r), (g3_s, g3_r)
+        place, shards, chunks, gather_turned, gather_order, own_sem, (gz_s, gz_r), (g2_s, g2_r), (g3_s, g3_r),
+        (gt_s, gt_r),
     )
     scatter = Scatter(
-        place, buffers, grads, scatter_order(pairs), first, mid_send, mid, last_send, last,
+        place, buffers, grads, scatter_turned, scatter_order, first, mid_send, mid, last_send, last,
         (s1_s, s1_r), (s2_s, s2_r), (sz_s, sz_r),
     )
 
@@ -726,11 +816,9 @@
     def layer_put(i):
         return pltpu.make_async_copy(stage.at[0, near(i)], layer_out.at[own_block(i)], out_sem.at[i])
 
-    gather.start(0)
+    gather.begin()
     for copy in (token_own, token_sent, cot_own, cot_sent):
         copy.start()
-    for c in range(1, count):
-        gather.start(c)
     sums[...] = jnp.zeros_like(sums)
     unit_sums[...] = jnp.zeros_like(unit_sums)
     head_sums[...] = jnp.zeros_like(head_sums)
@@ -757,6 +845,7 @@
             made = dot_nn(token[at, :], wa[p]) + bias
             qkv[p, at, :] = made.astype(low_type)
             value_t[:, at] = made[:, 2 * pair :].T.astype(low_type)
+            key_t[p, :, at] = made[:, pair : 2 * pair].T.astype(low_type)
 
         pace = gather_pace[min(p, len(gather_pace) - 2)]
         gather.advance(pace[0])
@@ -991,14 +1080,9 @@
         hidden_swap(i).wait_send()
         layer_put(i).wait()
         layer_swap(i).wait()
-    key_t, query_t = pair_low, pair_wide
+    query_t = pair_wide
     bias_sums = []
     for p in range(pairs):
-
-        @pl.loop(0, blocks)
-        def _(b, p=p):
-            at = rows_at(b, rows)
-            key_t[:, at] = qkv[p, at, pair : 2 * pair].astype(wide).T.astype(low_type)
 
         key_grad[...] = jnp.zeros_like(key_grad)
         value_grad[...] = jnp.zeros_like(value_grad)
@@ -1028,7 +1112,7 @@
                     grad_score = (prob * (grad_prob - inner)).astype(low_type)
                     value_grad[at, :] += dot_nn(prob.astype(low_type), context)
                     key_grad[at, :] += dot_nn(grad_score, query)
-                    found = found + dot_nn(key_t[head_rows, at], grad_score)
+                    found = found + dot_nn(key_t[p, head_rows, at], grad_score)
                 query_t[head_rows, b * rows : (b + 1) * rows] = found * size ** (-0.5)
                 for now in range(2):
                     if b % 2 and pace[2 * now + b // 2]:
@@ -1043,31 +1127,28 @@
             at = pl.ds(b * rows, rows)
             query_low = query_t[:, at].T.astype(low_type)
             value_low = value_grad[at, :].astype(low_type)
-            triple[at, :pair] = query_low
-            triple[at, pair : 2 * pair] = key_grad[at, :].astype(low_type)
-            triple[at, 2 * pair :] = value_low
+            qkv[p, at, :pair] = query_low
+            qkv[p, at, pair : 2 * pair] = key_grad[at, :].astype(low_type)
+            qkv[p, at, 2 * pair :] = value_low
             query_sum += fold_rows(query_low.astype(wide))
             value_sum += fold_rows(value_low.astype(wide))
         bias_sums.append((query_sum, value_sum))
-        product(buffers[5 + p], token_t, triple)
+        product(buffers[5 + p], token_t, qkv.at[p])
         scatter.begin(5 + p)
         scatter.advance(pace[4])
 
-        @pl.loop(0, blocks)
-        def _(t, p=p):
-            b = mate_first(t)
-            at = rows_at(b, rows)
-            made = dot_nt(triple[at, :], wa[p])
-            if p > 0:
-                made = total[at, :] + made
-            if p < pairs - 1:
-                total[at, :] = made
-            else:
-                kept = second[rows_at(lax.rem(t, own_count), rows), :]
-                made = made + jnp.where(t >= own_count, kept, 0.0)
-                total[at, :part] = jnp.where(place.col == 0, made[:, part:], made[:, :part])
-                total[at, part:] = jnp.where(place.col == 0, made[:, :part], made[:, part:])
-                token_swap(b).start()
+    @pl.loop(0, blocks)
+    def _(t):
+        b = mate_first(t)
+        at = rows_at(b, rows)
+        made = dot_nt(qkv[0, at, :], wa[0])
+        for p in range(1, pairs):
+            made = made + dot_nt(qkv[p, at, :], wa[p])
+        kept = second[rows_at(lax.rem(t, own_count), rows), :]
+        made = made + jnp.where(t >= own_count, kept, 0.0)
+        total[at, :part] = jnp.where(place.col == 0, made[:, part:], made[:, :part])
+        total[at, part:] = jnp.where(place.col == 0, made[:, :part], made[:, part:])
+        token_swap(b).start()
 
     def whole(values):
         return jnp.sum(values, axis=0, keepdims=True)
@@ -1143,16 +1224,26 @@
         ).wait()
 
 
-def place_kernel(
-    cut,
-    small, down_0, down_1, up_0, up_1, grad_out_t, *rest,
-):
+def place_kernel(cut, layer_in, token_in, small, down_0, down_1, up_0, up_1, grad_out_t, *rest):
     pairs, pair, part, width = cut.heads // 2, 2 * cut.size, cut.part_width, cut.width
     pieces, rest = rest[:pairs], rest[pairs:]
     (
-        grad_qkv, grad_out, grad_up, grad_down, query_bias, value_bias, out_bias, up_bias, down_bias, first_gain,
-        first_shift, second_gain, second_shift, head, hidden, unit, attention, feedforward,
+        layer_out, token_out, grad_qkv, grad_out, grad_up, grad_down, query_bias, value_bias, out_bias, up_bias,
+        down_bias, first_gain, first_shift, second_gain, second_shift, head, hidden, unit, attention, feedforward,
+        held, in_sem, out_sem,
     ) = rest
+    count = held.shape[1]
+    step = layer_in.shape[0] // count
+    moves = []
+    for a, (source, target) in enumerate(((layer_in, layer_out), (token_in, token_out))):
+        for i in range(count):
+            at = pl.ds(i * step, step)
+            into = pltpu.make_async_copy(source.at[at], held.at[a, i], in_sem.at[a, i])
+            into.start()
+            moves.append((into, pltpu.make_async_copy(held.at[a, i], target.at[at], out_sem.at[a, i])))
+    for into, out in moves:
+        into.wait()
+        out.start()
     group = cut.units // 2
     for p, piece in enumerate(pieces):
         for k in range(3):
@@ -1181,18 +1272,16 @@
     seq_total = attention.shape[0]
     flat(attention, small[7:8, :seq_total])
     flat(feedforward, small[7:8, width // 2 : width // 2 + seq_total])
-
-
-def gather_order(count):
-    return [(stage, t - stage) for t in range(count + 2) for stage in range(3) if 0 <= t - stage < count]
-
-
-def scatter_order(pairs):
-    return [(0, 0), (0, 1), (1, 0), (0, 2), (1, 1), (2, 0), (0, 3), (0, 4), (1, 2), (2, 1), (0, 5), (1, 3), (1, 5), (0, 6), (1, 4), (0, 7), (2, 2), (1, 6), (2, 3), (1, 7), (2, 5), (2, 4), (2, 6), (2, 7)]
-
-
-gather_pace = ((1, 1, 0, 1, 0), (1, 1, 1, 1, 1), (1, 0, 1, 0, 1), (1, 1))
-scatter_pace = ((1, 1), (0, 0), (0,), (1, 0, 0, 1, 0), (2, 1, 1, 1, 0), (1, 2, 0, 0, 1))
+    for _, out in moves:
+        out.wait()
+
+
+gather_turned = (5, 7)
+scatter_turned = (0,)
+gather_order = ((-1, 0), (-1, 1), (0, 0), (-1, 2), (0, 1), (-1, 3), (1, 0), (0, 2), (-1, 4), (1, 1), (2, 0), (0, 3), (-1, 5), (1, 2), (2, 1), (0, 4), (-1, 6), (1, 3), (2, 2), (0, 5), (-1, 7), (1, 4), (2, 3), (0, 6), (1, 5), (2, 4), (0, 7), (1, 6), (2, 5), (1, 7), (2, 6), (2, 7))
+scatter_order = ((0, 0), (0, 1), (0, 2), (1, 0), (1, 1), (0, 3), (0, 4), (1, 2), (2, 0), (0, 5), (1, 3), (1, 4), (0, 6), (1, 5), (0, 7), (1, 6), (2, 1), (1, 7), (2, 3), (2, 4), (2, 6), (2, 5), (2, 2), (2, 7))
+gather_pace = ((3, 0, 0, 0, 3), (1, 3, 0, 0, 1), (0, 0, 1, 3, 2), (0, 2))
+scatter_pace = ((0, 1), (0, 1), (0,), (1, 0, 0, 1, 1), (1, 1, 1, 1, 0), (1, 1, 1, 2, 0))
 
 
 class Cut(NamedTuple):
@@ -1268,11 +1357,11 @@
         ((2, length // 2, half), wide),
         ((length, half), wide),
         ((length, half), low_type),
-        ((length, half), low_type),
         ((length, 2 * cut.size), wide),
         ((length, 2 * cut.size), wide),
         ((2 * cut.size, length), wide),
         ((2 * cut.size, length), low_type),
+        ((pairs, 2 * cut.size, length), low_type),
         ((pairs + 1, cut.part, half), low_type),
         ((4, cut.part, group), low_type),
         ((16, width), wide),
@@ -1285,14 +1374,16 @@
     ]
     quarter = cut.part * cut.row_size // 2
     own += [((width, n), low_type) for n in columns]
-    own += [((2, 2, quarter, n), low_type) for n in columns]
-    own += [((2, quarter, n), low_type) for n in columns]
-    own += [((2, quarter, n), low_type) for n in columns]
-    own += [((2 * quarter, n), low_type) for n in columns]
-    own += [((cut.row_size - 1, cut.part, n), low_type) for n in columns]
     z = cut.row_size - 1
+    turned = [c in scatter_turned for c in range(count)]
+    both = list(zip(columns, turned))
+    own += [((2, 2, 2 * quarter, n // 2) if turn else (2, 2, quarter, n), low_type) for n, turn in both]
+    own += [((4, 2 * quarter, n // 2) if turn else (2, quarter, n), low_type) for n, turn in both]
+    own += [((z, 4, cut.part, n // 2) if turn else (2, quarter, n), low_type) for n, turn in both]
+    own += [((2, cut.part, n // 2) if turn else (2 * quarter, n), low_type) for n, turn in both]
+    own += [((2, cut.part, n // 2) if turn else (z, cut.part, n), low_type) for n, turn in both]
     semaphores = [dma(count), dma(count, z), dma(count, z), dma(count, 2), dma(count, 2), dma(count, 4), dma(count, 4)]
-    semaphores += [dma(2), dma(blocks // 2 + blocks)]
+    semaphores += [dma(count, 2 * z), dma(count, 2 * z), dma(2), dma(blocks // 2 + blocks)]
     semaphores += [dma(count, 4), dma(count, 4), dma(count, 2), dma(count, 2), dma(count, z), dma(count, z)]
     pair_swaps = 3 + 7 * (blocks // 2) + blocks
     semaphores += [dma(pair_swaps), dma(pair_swaps), dma(2 + z), dma(2 + z)]
@@ -1320,15 +1411,17 @@
     ]
     scalars = [head_gate, attention_gate, feedforward_gate, prefix_length]
     weights = [qkv_weight, out_weight.T, up_weight, down_weight.T]
-    layer_out, grad_tokens, *made = run_layer(cut, tokens, cotangent, *weights, *rows, *scalars)
+    made = run_layer(cut, tokens, cotangent, *weights, *rows, *scalars)
     seq_total = lax.axis_size(("dp", "row"))
     lanes = [half, half, width, units, width, width, width, width, width, cut.heads, width, units, seq_total, seq_total]
     shapes = [(3, part, half), (part, half), (part, units), (part, units)] + [(n,) for n in lanes]
-    outs = pl.pallas_call(
+    whole = (cut.length, half)
+    layer_out, grad_tokens, *outs = pl.pallas_call(
         partial(place_kernel, cut),
-        out_shape=like([(shape, wide) for shape in shapes]),
-        in_specs=[vmem_spec()] * len(made),
-        out_specs=[vmem_spec()] * len(shapes),
+        out_shape=like([(shape, wide) for shape in [whole, whole] + shapes]),
+        in_specs=[any_spec()] * 2 + [vmem_spec()] * (len(made) - 2),
+        out_specs=[any_spec()] * 2 + [vmem_spec()] * len(shapes),
+        scratch_shapes=[pltpu.VMEM((2, 4, cut.length // 4, half), wide), dma(2, 4), dma(2, 4)],
         name="place_results",
     )(*made)
     return (layer_out, grad_tokens, outs[0], outs[1].T, outs[2], outs[3].T, *outs[4:])

time: 171 us -> 162 us (0.947)
  Pallas kernels: 164 us -> 159 us
  local copies, waits for them, and re-layouts: 3.92 us -> 0 us
    pallas_call x1, Pallas kernels: 162 us -> 154 us  [run_layer(): pl.pallas_call(partial(layer_kernel, cut), out_shape=like(outs), in_specs...]
    unnamed x4 -> x0, local copies, waits for them, and re-layouts: 3.92 us -> none
    pallas_call x1, Pallas kernels: 2.24 us -> 5.05 us  [fused_device(): pl.pallas_call(partial(place_kernel, cut), out_shape=like([(shape, wide)...]
where the time goes in v2:
time: 162 us
  Pallas kernels  159 us (98%)
  between operations  2.79 us (2%)
    pallas_call x1, Pallas kernels, run_layer(): pl.pallas_call(partial(layer_kernel, cut), out_shape=like(outs), in_specs...  154 us
    pallas_call x1, Pallas kernels, fused_device(): pl.pallas_call(partial(place_kernel, cut), out_shape=like([(shape, wide)...  5.05 us

profile of v2, /device:TPU:0, one launch (start us, length us, event | category | flops | bytes accessed | tf_op | source)
XLA Modules:
  0.0 161.9 jit_solution(3196918793540933566)
XLA Ops:
  2.6 154.1 %whole_layer.1 = (f32[1024,384]{1,0:T(8,128)}, f32[1024,384]{1,0:T(8,128)}, f32[16,768]{1,0:T(8,128)}, f32[48,768]{1,0:T(8,128)}, f32[48,768]{1,0:T(8,128)}, /*i...) custom-call(bf16[1024,384]{1,0:T(8,128)(2,1)} %token_part.1, ...), custom_call_target="tpu_custom_call" | custom-call | tf_op jit(solution)/shard_map/whole_layer/pallas_call | solution.py:1390
  156.7 5.0 %place_results.1 = (f32[1024,384]{1,0:T(8,128)}, f32[1024,384]{1,0:T(8,128)}, f32[3,48,384]{2,1,0:T(8,128)}, f32[48,384]{1,0:T(8,128)}, f32[48,1536]{1,0:T(8,128...) custom-call(f32[1024,384]{1,0:T(8,128)} %get-tuple-element.51.layer_, ...), custom_call_target="tpu_custom_call" | custom-call | tf_op jit(solution)/shard_map/place_results/pallas_call | solution.py:1419

commit v3 on v2

--- a/solution.py
+++ b/solution.py
@@ -1224,30 +1224,36 @@
         ).wait()
 
 
-def place_kernel(cut, layer_in, token_in, small, down_0, down_1, up_0, up_1, grad_out_t, *rest):
+def place_kernel(cut, count, layer_in, token_in, *rest):
     pairs, pair, part, width = cut.heads // 2, 2 * cut.size, cut.part_width, cut.width
-    pieces, rest = rest[:pairs], rest[pairs:]
+    sources, rest = rest[:count], rest[count:]
     (
         layer_out, token_out, grad_qkv, grad_out, grad_up, grad_down, query_bias, value_bias, out_bias, up_bias,
         down_bias, first_gain, first_shift, second_gain, second_shift, head, hidden, unit, attention, feedforward,
-        held, in_sem, out_sem,
-    ) = rest
-    count = held.shape[1]
-    step = layer_in.shape[0] // count
+    ) = rest[:20]
+    held, targets, (in_sem, out_sem, source_sem) = rest[20], rest[21 : 21 + count], rest[21 + count :]
+    parts = held.shape[1]
+    step = layer_in.shape[0] // parts
     moves = []
     for a, (source, target) in enumerate(((layer_in, layer_out), (token_in, token_out))):
-        for i in range(count):
+        for i in range(parts):
             at = pl.ds(i * step, step)
             into = pltpu.make_async_copy(source.at[at], held.at[a, i], in_sem.at[a, i])
             into.start()
             moves.append((into, pltpu.make_async_copy(held.at[a, i], target.at[at], out_sem.at[a, i])))
+    loads = [pltpu.make_async_copy(a, b, source_sem.at[i]) for i, (a, b) in enumerate(zip(sources, targets))]
+    for copy in loads:
+        copy.start()
     for into, out in moves:
         into.wait()
         out.start()
+    for copy in loads:
+        copy.wait()
+    small, down_0, down_1, up_0, up_1, grad_out_t, *pieces = targets
     group = cut.units // 2
-    for p, piece in enumerate(pieces):
+    for p in range(pairs):
         for k in range(3):
-            grad_qkv[k, :, p * pair : (p + 1) * pair] = piece[:, k * pair : (k + 1) * pair]
+            grad_qkv[k, :, p * pair : (p + 1) * pair] = pieces[p][:, k * pair : (k + 1) * pair]
     grad_out[...] = grad_out_t[...]
     for j, (up, down) in enumerate(((up_0, down_0), (up_1, down_1))):
         grad_up[:, j * group : (j + 1) * group] = up[...]
@@ -1279,7 +1285,7 @@
 gather_turned = (5, 7)
 scatter_turned = (0,)
 gather_order = ((-1, 0), (-1, 1), (0, 0), (-1, 2), (0, 1), (-1, 3), (1, 0), (0, 2), (-1, 4), (1, 1), (2, 0), (0, 3), (-1, 5), (1, 2), (2, 1), (0, 4), (-1, 6), (1, 3), (2, 2), (0, 5), (-1, 7), (1, 4), (2, 3), (0, 6), (1, 5), (2, 4), (0, 7), (1, 6), (2, 5), (1, 7), (2, 6), (2, 7))
-scatter_order = ((0, 0), (0, 1), (0, 2), (1, 0), (1, 1), (0, 3), (0, 4), (1, 2), (2, 0), (0, 5), (1, 3), (1, 4), (0, 6), (1, 5), (0, 7), (1, 6), (2, 1), (1, 7), (2, 3), (2, 4), (2, 6), (2, 5), (2, 2), (2, 7))
+scatter_order = ((0, 0), (0, 1), (0, 2), (1, 0), (1, 1), (0, 3), (0, 4), (1, 2), (0, 5), (2, 0), (1, 3), (1, 4), (0, 6), (1, 5), (0, 7), (1, 6), (2, 1), (1, 7), (2, 3), (2, 4), (2, 6), (2, 5), (2, 2), (2, 7))
 gather_pace = ((3, 0, 0, 0, 3), (1, 3, 0, 0, 1), (0, 0, 1, 3, 2), (0, 2))
 scatter_pace = ((0, 1), (0, 1), (0,), (1, 0, 0, 1, 1), (1, 1, 1, 1, 0), (1, 1, 1, 2, 0))
 
@@ -1416,12 +1422,14 @@
     lanes = [half, half, width, units, width, width, width, width, width, cut.heads, width, units, seq_total, seq_total]
     shapes = [(3, part, half), (part, half), (part, units), (part, units)] + [(n,) for n in lanes]
     whole = (cut.length, half)
+    held = [((2, 4, cut.length // 4, half), wide)] + [(piece.shape, piece.dtype) for piece in made[2:]]
+    count = len(made) - 2
     layer_out, grad_tokens, *outs = pl.pallas_call(
-        partial(place_kernel, cut),
+        partial(place_kernel, cut, count),
         out_shape=like([(shape, wide) for shape in [whole, whole] + shapes]),
-        in_specs=[any_spec()] * 2 + [vmem_spec()] * (len(made) - 2),
+        in_specs=[any_spec()] * len(made),
         out_specs=[any_spec()] * 2 + [vmem_spec()] * len(shapes),
-        scratch_shapes=[pltpu.VMEM((2, 4, cut.length // 4, half), wide), dma(2, 4), dma(2, 4)],
+        scratch_shapes=scratch(held) + [dma(2, 4), dma(2, 4), dma(count)],
         name="place_results",
     )(*made)
     return (layer_out, grad_tokens, outs[0], outs[1].T, outs[2], outs[3].T, *outs[4:])

time: 162 us -> 161 us (level)
  no operation moved by 1% of the time
where the time goes in v3:
time: 161 us
  Pallas kernels  158 us (98%)
  between operations  2.79 us (2%)
    pallas_call x1, Pallas kernels, run_layer(): pl.pallas_call(partial(layer_kernel, cut), out_shape=like(outs), in_specs...  154 us
    pallas_call x1, Pallas kernels, fused_device(): pl.pallas_call(partial(place_kernel, cut, count), out_shape=like([(shape,...  4.58 us

profile of v3, /device:TPU:0, one launch (start us, length us, event | category | flops | bytes accessed | tf_op | source)
XLA Modules:
  0.0 161.1 jit_solution(13733567318013680111)
XLA Ops:
  2.6 153.8 %whole_layer.1 = (f32[1024,384]{1,0:T(8,128)}, f32[1024,384]{1,0:T(8,128)}, f32[16,768]{1,0:T(8,128)}, f32[48,768]{1,0:T(8,128)}, f32[48,768]{1,0:T(8,128)}, /*i...) custom-call(bf16[1024,384]{1,0:T(8,128)(2,1)} %token_part.1, ...), custom_call_target="tpu_custom_call" | custom-call | tf_op jit(solution)/shard_map/whole_layer/pallas_call | solution.py:1396
  156.4 4.6 %place_results.1 = (f32[1024,384]{1,0:T(8,128)}, f32[1024,384]{1,0:T(8,128)}, f32[3,48,384]{2,1,0:T(8,128)}, f32[48,384]{1,0:T(8,128)}, f32[48,1536]{1,0:T(8,128...) custom-call(f32[1024,384]{1,0:T(8,128)} %get-tuple-element.51.layer_, ...), custom_call_target="tpu_custom_call" | custom-call | tf_op jit(solution)/shard_map/place_results/pallas_call | solution.py:1427

commit v4 on v3

--- a/solution.py
+++ b/solution.py
@@ -603,7 +603,15 @@
         self.done += 1
         if c in self.turned:
             self.turned_step(stage, c)
-            return
+        else:
+            self.plain_step(stage, c)
+        if stage == 2:
+            self.put(c).start()
+
+    def put(self, c):
+        return pltpu.make_async_copy(self.outs[c], self.results[c], self.put_sem.at[c])
+
+    def plain_step(self, stage, c):
         place, chunk = self.place, self.chunks[c]
         first, mid_send, mid = self.first[c], self.mid_send[c], self.mid[c]
         last_send, last = self.last_send[c], self.last[c]
@@ -679,6 +687,7 @@
         for c in range(self.count):
             for copy in self.one(c) + self.two(c) + self.along_z(c):
                 copy.wait_send()
+            self.put(c).wait()
 
 
 def masked_tile(tile, query_start, key_start, prefix):
@@ -725,15 +734,16 @@
         del rest[:number]
         return taken
 
-    grads = take(count)
+    results = take(count)
     (wa, wm, token, token_t, qkv, lse, ctx, attn_out, normed_t, gelu, slope, second, low, dense_t, sums) = take(15)
     (cot, total, arrive_a, arrive_b, stage, token_recv, ctx_grad, key_grad, value_grad) = take(9)
     (pair_wide, pair_low, key_t, shards_a, shards_m) = take(5)
+    grads = take(count)
     (small, small_c, small_x, small_y, small_z, unit_sums, head_sums) = take(7)
     buffers, first, mid_send, mid, last_send, last = (take(count) for _ in range(6))
     (own_sem, gz_s, gz_r, g2_s, g2_r, g3_s, g3_r, gt_s, gt_r, half_sem, out_sem) = take(11)
     (s1_s, s1_r, s2_s, s2_r, sz_s, sz_r) = take(6)
-    (col_s, col_r, small_s, small_r) = take(4)
+    (col_s, col_r, small_s, small_r, put_sem) = take(5)
     group = wm.shape[2]
     place = Place(cut.row_size)
     for p in range(pairs):
@@ -763,6 +773,7 @@
         place, buffers, grads, scatter_turned, scatter_order, first, mid_send, mid, last_send, last,
         (s1_s, s1_r), (s2_s, s2_r), (sz_s, sz_r),
     )
+    scatter.results, scatter.put_sem = results, put_sem
 
     def to_mate(source, target, index):
         return send(source, target, (col_s, col_r), index, place.col_mate())
@@ -1370,6 +1381,7 @@
         ((pairs, 2 * cut.size, length), low_type),
         ((pairs + 1, cut.part, half), low_type),
         ((4, cut.part, group), low_type),
+        *[((cut.part, n), wide) for n in columns],
         ((16, width), wide),
         ((2, 16, width), wide),
         ((2, 16, width), wide),
@@ -1392,12 +1404,12 @@
     semaphores += [dma(count, 2 * z), dma(count, 2 * z), dma(2), dma(blocks // 2 + blocks)]
     semaphores += [dma(count, 4), dma(count, 4), dma(count, 2), dma(count, 2), dma(count, z), dma(count, z)]
     pair_swaps = 3 + 7 * (blocks // 2) + blocks
-    semaphores += [dma(pair_swaps), dma(pair_swaps), dma(2 + z), dma(2 + z)]
+    semaphores += [dma(pair_swaps), dma(pair_swaps), dma(2 + z), dma(2 + z), dma(count)]
     return pl.pallas_call(
         partial(layer_kernel, cut),
         out_shape=like(outs),
         in_specs=[any_spec()] * 2 + [vmem_spec()] * (len(args) - 6) + [smem_spec()] * 4,
-        out_specs=[any_spec()] * 2 + [vmem_spec()] * (len(outs) - 2),
+        out_specs=[any_spec()] * 2 + [vmem_spec()] + [any_spec()] * count,
         scratch_shapes=scratch(own) + semaphores,
         compiler_params=pltpu.CompilerParams(collective_id=0, has_side_effects=True, vmem_limit_bytes=vmem_most),
         name="whole_layer",

time: 161 us -> 162 us (level)
  no operation moved by 1% of the time
where the time goes in v4:
time: 162 us; the launch traced here: 161 us
  Pallas kernels  159 us (98%)
  between operations  2.79 us (2%)
    pallas_call x1, Pallas kernels, run_layer(): pl.pallas_call(partial(layer_kernel, cut), out_shape=like(outs), in_specs...  154 us
    pallas_call x1, Pallas kernels, fused_device(): pl.pallas_call(partial(place_kernel, cut, count), out_shape=like([(shape,...  4.58 us

profile of v4, /device:TPU:0, one launch (start us, length us, event | category | flops | bytes accessed | tf_op | source)
XLA Modules:
  0.0 161.4 jit_solution(14387195625411623265)
XLA Ops:
  2.6 154.0 %whole_layer.1 = (f32[1024,384]{1,0:T(8,128)}, f32[1024,384]{1,0:T(8,128)}, f32[16,768]{1,0:T(8,128)}, f32[48,768]{1,0:T(8,128)}, f32[48,768]{1,0:T(8,128)}, /*i...) custom-call(bf16[1024,384]{1,0:T(8,128)(2,1)} %token_part.1, ...), custom_call_target="tpu_custom_call" | custom-call | tf_op jit(solution)/shard_map/whole_layer/pallas_call | solution.py:1408
  156.7 4.6 %place_results.1 = (f32[1024,384]{1,0:T(8,128)}, f32[1024,384]{1,0:T(8,128)}, f32[3,48,384]{2,1,0:T(8,128)}, f32[48,384]{1,0:T(8,128)}, f32[48,1536]{1,0:T(8,128...) custom-call(f32[1024,384]{1,0:T(8,128)} %get-tuple-element.51.layer_, ...), custom_call_target="tpu_custom_call" | custom-call | tf_op jit(solution)/shard_map/place_results/pallas_call | solution.py:1439
